TPU v7x, 256 devices: a whole 4x4x8 slice. The times are simulated.
256 devices in a mesh: gx: 16 (over z, core), yz: 16 (over y, x).
Axes of the slice: x: 4, y: 4, z: 8, core: 2. Of those that a mesh axis runs over, the one named last changes fastest.
Arguments:
- state: float32 [5, 256, 256, 256], P(None, 'gx', 'yz'), may hold values from -3 to 9, as said below
- register: float32 [5, 256, 256, 256], P(None, 'gx', 'yz'), may hold values from -4 to 4
Outputs:
- register_out: float32 [5, 256, 256, 256], P(None, 'gx', 'yz')
- filtered: float32 [5, 256, 256, 256], P(None, 'gx', 'yz')
Inputs may be any that keep to these rules, and one draw needn't show every extreme that they name: state holds the density, the three momenta and the total energy of an ideal gas with ratio of specific heats 1.4; in every cell the density lies between 0.4 and 2.2 and the pressure between 0.4 and 2.1.
All inputs are finite; a program needn't handle non-finite values.
Results may differ from a plain program's by a relative error of at most 0.0003.
Values sent between devices are 32-bit elements; how exact they have to be, the bound alone decides.
No kernel may reach another device: no remote copies, remote signals or barrier semaphores. Data moves between devices by JAX's collectives and lax.ppermute only.
A program may use at most 128 MiB of HBM per device.

v0:
```python
import jax
import jax.numpy as jnp
from jax import lax
from jax.sharding import PartitionSpec as P

gamma_gas = 1.4
central_weights = (4.0 / 5.0, -1.0 / 5.0, 4.0 / 105.0, -1.0 / 280.0)
filter_alpha = 0.49
register_decay = -5.0 / 9.0
register_gain = 15.0 / 16.0
time_step = 0.2


def with_halo(cells, sides, width):
    for axis, dim in sides:
        count = lax.axis_size(axis)
        head = lax.slice_in_dim(cells, 0, width, axis=dim)
        tail = lax.slice_in_dim(cells, cells.shape[dim] - width, cells.shape[dim], axis=dim)
        cells = jnp.concatenate(
            [
                lax.ppermute(tail, axis, [(i, (i + 1) % count) for i in range(count)]),
                cells,
                lax.ppermute(head, axis, [((i + 1) % count, i) for i in range(count)]),
            ],
            axis=dim,
        )
    return cells


def primitives(fields):
    density = fields[0]
    speed_x = fields[1] / density
    speed_y = fields[2] / density
    speed_z = fields[3] / density
    kinetic = 0.5 * density * (speed_x * speed_x + speed_y * speed_y + speed_z * speed_z)
    pressure = (gamma_gas - 1.0) * (fields[4] - kinetic)
    enthalpy = (fields[4] + pressure) / density
    return (density, speed_x, speed_y, speed_z, pressure, enthalpy)


def pair_flux(left, right, direction):
    means = [0.5 * (one + other) for one, other in zip(left, right)]
    density, speed_x, speed_y, speed_z, pressure, enthalpy = means
    normal = (speed_x, speed_y, speed_z)[direction]
    mass = density * normal
    moment = [mass * speed_x, mass * speed_y, mass * speed_z]
    moment[direction] = moment[direction] + pressure
    return [mass] + moment + [mass * enthalpy]


def residual_of(padded):
    width_x = padded.shape[1] - 8
    width_y = padded.shape[2] - 8
    along_x = primitives(padded[:, :, 4:-4])
    along_y = primitives(padded[:, 4:-4, :])
    center = tuple((column[4:-4] for column in along_x))
    total = [jnp.zeros_like(center[0]) for field in range(5)]
    for offset in range(1, 5):
        weight = central_weights[offset - 1]
        left = tuple((column[:-offset] for column in along_x))
        right = tuple((column[offset:] for column in along_x))
        flux = pair_flux(left, right, 0)
        total = [
            part
            - 2.0 * weight * (value[4 : 4 + width_x] - value[4 - offset : 4 - offset + width_x])
            for part, value in zip(total, flux)
        ]
    for offset in range(1, 5):
        weight = central_weights[offset - 1]
        left = tuple((column[:, :-offset] for column in along_y))
        right = tuple((column[:, offset:] for column in along_y))
        flux = pair_flux(left, right, 1)
        total = [
            part
            - 2.0
            * weight
            * (value[:, 4 : 4 + width_y] - value[:, 4 - offset : 4 - offset + width_y])
            for part, value in zip(total, flux)
        ]
    for offset in range(1, 5):
        weight = central_weights[offset - 1]
        ahead = tuple((jnp.roll(column, -offset, axis=2) for column in center))
        flux = pair_flux(center, ahead, 2)
        total = [
            part - 2.0 * weight * (value - jnp.roll(value, offset, axis=2))
            for part, value in zip(total, flux)
        ]
    return jnp.stack(total)


def filter_rhs(extended):
    coeffs = (
        (11.0 + 10.0 * filter_alpha) / 16.0,
        (15.0 + 34.0 * filter_alpha) / 32.0,
        (-3.0 + 6.0 * filter_alpha) / 16.0,
        (1.0 - 2.0 * filter_alpha) / 32.0,
    )
    width_x = extended.shape[1] - 6
    rhs = coeffs[0] * extended[:, 3 : 3 + width_x]
    for shift in range(1, 4):
        rhs = rhs + coeffs[shift] / 2.0 * (
            extended[:, 3 + shift : 3 + shift + width_x]
            + extended[:, 3 - shift : 3 - shift + width_x]
        )
    return rhs


def line_solve(rhs, own):
    highest = lax.Precision.HIGHEST
    inner = rhs.shape[1] - 1
    places = jnp.arange(inner)
    lower = jnp.where(places == 0, 0.0, filter_alpha).astype(jnp.float32)
    upper = jnp.where(places == inner - 1, 0.0, filter_alpha).astype(jnp.float32)
    middle = jnp.ones((inner,), jnp.float32)
    inverse = lax.linalg.tridiagonal_solve(lower, middle, upper, jnp.eye(inner, dtype=jnp.float32))
    interior = jnp.einsum("ij,fjyz->fiyz", inverse, rhs[:, :inner], precision=highest)
    first = interior[:, 0]
    partial_rhs = rhs[:, inner] - filter_alpha * interior[:, inner - 1]
    pairs = jnp.stack([first, partial_rhs])[None]
    count = pairs.shape[0]
    coupled = pairs[:, 1] - filter_alpha * jnp.roll(pairs[:, 0], -1, axis=0)
    diagonal = 1.0 - 2.0 * filter_alpha * filter_alpha * inverse[0, 0]
    across = -filter_alpha * filter_alpha * inverse[inner - 1, 0]
    cycle = jnp.arange(count)
    following = (cycle[None, :] == (cycle[:, None] + 1) % count).astype(jnp.float32)
    system = diagonal * jnp.eye(count, dtype=jnp.float32) + across * (following + following.T)
    factor = jnp.linalg.cholesky(system)
    system_inverse = jax.scipy.linalg.cho_solve((factor, True), jnp.eye(count, dtype=jnp.float32))
    before_row = lax.dynamic_index_in_dim(
        system_inverse, (own + count - 1) % count, 0, keepdims=False
    )
    own_row = lax.dynamic_index_in_dim(system_inverse, own, 0, keepdims=False)
    rows = jnp.stack([before_row, own_row])
    separators = jnp.einsum("kp,pfyz->kfyz", rows, coupled, precision=highest)
    before_sep = separators[0]
    own_sep = separators[1]
    solved = interior - filter_alpha * (
        before_sep[:, None] * inverse[:, 0][None, :, None, None]
        + own_sep[:, None] * inverse[:, inner - 1][None, :, None, None]
    )
    return jnp.concatenate([solved, own_sep[:, None]], axis=1)


def body(state, register):
    padded = with_halo(state, (("gx", 1), ("yz", 2)), 4)
    residual = residual_of(padded)
    register_out = register_decay * register + time_step * residual
    section = state + register_gain * register_out
    extended = with_halo(section, (("gx", 1),), 3)
    rhs = filter_rhs(extended)
    solved = line_solve(lax.all_to_all(rhs, "gx", split_axis=3, concat_axis=1, tiled=True), 0)
    filtered = lax.all_to_all(solved, "gx", split_axis=1, concat_axis=3, tiled=True)
    return (register_out, filtered)


def solution(mesh):
    in_specs = (P(None, "gx", "yz", None), P(None, "gx", "yz", None))
    out_specs = (P(None, "gx", "yz", None), P(None, "gx", "yz", None))
    return jax.shard_map(body, mesh=mesh, in_specs=in_specs, out_specs=out_specs, check_vma=False)
```

profile of v0, /device:TPU:1, one launch (start us, length us, event | category | flops | bytes accessed | tf_op | source)
XLA Modules:
  0.0 920.2 jit_solution(6486800691322483803)
XLA Ops:
  9.9 473.2 %while.32 = (s32[]{:T(128)}, f32[]{:T(128)}, f32[255]{0:T(256)S(1)}, f32[7,32]{1,0:T(8,128)}, f32[7,32,255]{2,1,0:T(8,128)S(1)}, /*index=5*/f32[7,32]{1,0:T(8,12...) while((s32[]{:T(128)}, f32[]{:T(128)}, ...), condition=%wide.region_1.2_spmd, body=%wide.region_0.1_spmd.sunk | while | flops 24609 | bytes 268269 | solution.py:115
  55.4 20.1 %subtract_divide_fusion.123 = (f32[255]{0:T(256)S(1)}, f32[255]{0:T(256)S(1)}, f32[255]{0:T(256)S(1)}, f32[255]{0:T(256)S(1)}, f32[255]{0:T(256)S(1)}, /*index=5...) fusion(f32[255]{0:T(256)S(1)} %bitcast.1298, ...), kind=kLoop, calls=%fused_computation.35.clone.1 | loop fusion | flops 24480 | bytes 66556 | tf_op jit(solution)/shard_map/while/body/eval_jaxpr/div | solution.py:115
  123.0 20.1 %subtract_divide_fusion.123 = (f32[255]{0:T(256)S(1)}, f32[255]{0:T(256)S(1)}, f32[255]{0:T(256)S(1)}, f32[255]{0:T(256)S(1)}, f32[255]{0:T(256)S(1)}, /*index=5...) fusion(f32[255]{0:T(256)S(1)} %bitcast.1298, ...), kind=kLoop, calls=%fused_computation.35.clone.1 | loop fusion | flops 24480 | bytes 66556 | tf_op jit(solution)/shard_map/while/body/eval_jaxpr/div | solution.py:115
  190.6 20.1 %subtract_divide_fusion.123 = (f32[255]{0:T(256)S(1)}, f32[255]{0:T(256)S(1)}, f32[255]{0:T(256)S(1)}, f32[255]{0:T(256)S(1)}, f32[255]{0:T(256)S(1)}, /*index=5...) fusion(f32[255]{0:T(256)S(1)} %bitcast.1298, ...), kind=kLoop, calls=%fused_computation.35.clone.1 | loop fusion | flops 24480 | bytes 66556 | tf_op jit(solution)/shard_map/while/body/eval_jaxpr/div | solution.py:115
  258.2 20.1 %subtract_divide_fusion.123 = (f32[255]{0:T(256)S(1)}, f32[255]{0:T(256)S(1)}, f32[255]{0:T(256)S(1)}, f32[255]{0:T(256)S(1)}, f32[255]{0:T(256)S(1)}, /*index=5...) fusion(f32[255]{0:T(256)S(1)} %bitcast.1298, ...), kind=kLoop, calls=%fused_computation.35.clone.1 | loop fusion | flops 24480 | bytes 66556 | tf_op jit(solution)/shard_map/while/body/eval_jaxpr/div | solution.py:115
  325.8 20.1 %subtract_divide_fusion.123 = (f32[255]{0:T(256)S(1)}, f32[255]{0:T(256)S(1)}, f32[255]{0:T(256)S(1)}, f32[255]{0:T(256)S(1)}, f32[255]{0:T(256)S(1)}, /*index=5...) fusion(f32[255]{0:T(256)S(1)} %bitcast.1298, ...), kind=kLoop, calls=%fused_computation.35.clone.1 | loop fusion | flops 24480 | bytes 66556 | tf_op jit(solution)/shard_map/while/body/eval_jaxpr/div | solution.py:115
  393.4 20.1 %subtract_divide_fusion.123 = (f32[255]{0:T(256)S(1)}, f32[255]{0:T(256)S(1)}, f32[255]{0:T(256)S(1)}, f32[255]{0:T(256)S(1)}, f32[255]{0:T(256)S(1)}, /*index=5...) fusion(f32[255]{0:T(256)S(1)} %bitcast.1298, ...), kind=kLoop, calls=%fused_computation.35.clone.1 | loop fusion | flops 24480 | bytes 66556 | tf_op jit(solution)/shard_map/while/body/eval_jaxpr/div | solution.py:115
  460.9 20.1 %subtract_divide_fusion.123 = (f32[255]{0:T(256)S(1)}, f32[255]{0:T(256)S(1)}, f32[255]{0:T(256)S(1)}, f32[255]{0:T(256)S(1)}, f32[255]{0:T(256)S(1)}, /*index=5...) fusion(f32[255]{0:T(256)S(1)} %bitcast.1298, ...), kind=kLoop, calls=%fused_computation.35.clone.1 | loop fusion | flops 24480 | bytes 66556 | tf_op jit(solution)/shard_map/while/body/eval_jaxpr/div | solution.py:115
  501.5 5.7 collective-permute-done.2
  515.6 6.4 collective-permute-start.5
  560.9 18.9 %subtract_divide_fusion.32 = (f32[255]{0:T(256)S(1)}, f32[255]{0:T(256)S(1)}, f32[255]{0:T(256)S(1)}, f32[255]{0:T(256)S(1)}, f32[255]{0:T(256)S(1)}, /*index=5*...) fusion(f32[255]{0:T(256)S(1)} %bitcast.1451, ...), kind=kLoop, calls=%fused_computation.641 | loop fusion | flops 22950 | bytes 62460 | tf_op jit(solution)/shard_map/eval_jaxpr/div | solution.py:115
  583.8 5.5 copy.35
  589.4 8.0 reshape.451
  597.4 9.3 %all-to-all-start = ((f32[16,1,20480]{2,1,0:T(1,128)}), f32[16,1,20480]{2,1,0:T(1,128)S(1)}, u32[]{:S(2)}, u32[]{:S(2)}) async-start(f32[16,1,20480]{2,1,0:T(1,128)} %reshape.451), calls=%async_computation | async-start | bytes 2621440 | tf_op jit(solution)/shard_map/all_to_all | solution.py:151
  606.7 165.4 %while.33 = (s32[]{:T(128)}, f32[255]{0:T(256)S(1)}, f32[7,32,255]{2,1,0:T(8,128)S(1)}, f32[7,32,255]{2,1,0:T(8,128)}, f32[7,32]{1,0:T(8,128)S(1)}, /*index=5*/s...) while((s32[]{:T(128)}, f32[255]{0:T(256)S(1)}, ...), condition=%wide.region_3.4_spmd, body=%wide.region_2.3_spmd.sunk | while | flops 16354 | bytes 265941 | solution.py:115
  610.3 19.9 %multiply_subtract_fusion.124 = (f32[255]{0:T(256)S(1)}, f32[255]{0:T(256)S(1)}, f32[255]{0:T(256)S(1)}, f32[255]{0:T(256)S(1)}, f32[255]{0:T(256)S(1)}, /*index...) fusion(f32[255]{0:T(256)S(1)} %bitcast.1365, ...), kind=kLoop, calls=%fused_computation.101.clone.1 | loop fusion | flops 16320 | bytes 66428 | tf_op jit(solution)/shard_map/while/body/eval_jaxpr/sub | solution.py:115
  633.9 19.9 %multiply_subtract_fusion.124 = (f32[255]{0:T(256)S(1)}, f32[255]{0:T(256)S(1)}, f32[255]{0:T(256)S(1)}, f32[255]{0:T(256)S(1)}, f32[255]{0:T(256)S(1)}, /*index...) fusion(f32[255]{0:T(256)S(1)} %bitcast.1365, ...), kind=kLoop, calls=%fused_computation.101.clone.1 | loop fusion | flops 16320 | bytes 66428 | tf_op jit(solution)/shard_map/while/body/eval_jaxpr/sub | solution.py:115
  657.6 19.9 %multiply_subtract_fusion.124 = (f32[255]{0:T(256)S(1)}, f32[255]{0:T(256)S(1)}, f32[255]{0:T(256)S(1)}, f32[255]{0:T(256)S(1)}, f32[255]{0:T(256)S(1)}, /*index...) fusion(f32[255]{0:T(256)S(1)} %bitcast.1365, ...), kind=kLoop, calls=%fused_computation.101.clone.1 | loop fusion | flops 16320 | bytes 66428 | tf_op jit(solution)/shard_map/while/body/eval_jaxpr/sub | solution.py:115
  681.2 19.9 %multiply_subtract_fusion.124 = (f32[255]{0:T(256)S(1)}, f32[255]{0:T(256)S(1)}, f32[255]{0:T(256)S(1)}, f32[255]{0:T(256)S(1)}, f32[255]{0:T(256)S(1)}, /*index...) fusion(f32[255]{0:T(256)S(1)} %bitcast.1365, ...), kind=kLoop, calls=%fused_computation.101.clone.1 | loop fusion | flops 16320 | bytes 66428 | tf_op jit(solution)/shard_map/while/body/eval_jaxpr/sub | solution.py:115
  704.8 19.9 %multiply_subtract_fusion.124 = (f32[255]{0:T(256)S(1)}, f32[255]{0:T(256)S(1)}, f32[255]{0:T(256)S(1)}, f32[255]{0:T(256)S(1)}, f32[255]{0:T(256)S(1)}, /*index...) fusion(f32[255]{0:T(256)S(1)} %bitcast.1365, ...), kind=kLoop, calls=%fused_computation.101.clone.1 | loop fusion | flops 16320 | bytes 66428 | tf_op jit(solution)/shard_map/while/body/eval_jaxpr/sub | solution.py:115
  728.5 19.9 %multiply_subtract_fusion.124 = (f32[255]{0:T(256)S(1)}, f32[255]{0:T(256)S(1)}, f32[255]{0:T(256)S(1)}, f32[255]{0:T(256)S(1)}, f32[255]{0:T(256)S(1)}, /*index...) fusion(f32[255]{0:T(256)S(1)} %bitcast.1365, ...), kind=kLoop, calls=%fused_computation.101.clone.1 | loop fusion | flops 16320 | bytes 66428 | tf_op jit(solution)/shard_map/while/body/eval_jaxpr/sub | solution.py:115
  752.1 19.9 %multiply_subtract_fusion.124 = (f32[255]{0:T(256)S(1)}, f32[255]{0:T(256)S(1)}, f32[255]{0:T(256)S(1)}, f32[255]{0:T(256)S(1)}, f32[255]{0:T(256)S(1)}, /*index...) fusion(f32[255]{0:T(256)S(1)} %bitcast.1365, ...), kind=kLoop, calls=%fused_computation.101.clone.1 | loop fusion | flops 16320 | bytes 66428 | tf_op jit(solution)/shard_map/while/body/eval_jaxpr/sub | solution.py:115
  773.6 18.8 %multiply_subtract_fusion.33 = (f32[255]{0:T(256)S(1)}, f32[255]{0:T(256)S(1)}, f32[255]{0:T(256)S(1)}, f32[255]{0:T(256)S(1)}, f32[255]{0:T(256)S(1)}, /*index=...) fusion(f32[255]{0:T(256)S(1)} %bitcast.1481, ...), kind=kLoop, calls=%fused_computation.611 | loop fusion | flops 15300 | bytes 62340 | tf_op jit(solution)/shard_map/eval_jaxpr/sub | solution.py:115
  800.1 8.3 reshape.452
  808.4 12.7 %copy.36 = f32[5,16,16,16,16]{1,3,4,2,0:T(8,128)} copy(f32[5,16,16,16,16]{2,1,0,4,3:T(8,128)} %bitcast.1216) | data formatting | bytes 2621440 | tf_op jit(solution)/shard_map/all_to_all | solution.py:151
  821.1 7.3 all_to_all.29
  831.8 5.5 copy.38
  837.3 7.2 reshape.453
  844.5 41.3 %all_to_all.36 = f32[16,1,20480]{2,1,0:T(1,128)S(1)} all-to-all(f32[16,1,20480]{2,1,0:T(1,128)S(1)} %reshape.453), channel_id=1, replica_groups=mesh['gx'=16,'yz'=16] {'gx'}, dimensions={0} | all-to-all | bytes 2621440 | tf_op jit(solution)/shard_map/all_to_all | solution.py:152
  889.6 8.2 reshape.454
  897.8 13.9 %copy.39 = f32[5,16,16,16,16]{4,3,2,1,0:T(8,128)} copy(f32[5,16,16,16,16]{4,2,0,1,3:T(8,128)} %bitcast.1219) | data formatting | bytes 2621440 | tf_op jit(solution)/shard_map/all_to_all | solution.py:152
  911.7 8.2 all_to_all.33
  (365 shorter events, 125.8 us)
Async XLA Ops:
  2.7 482.9 %collective-permute-start = (f32[5,4,16,256]{3,2,1,0:T(8,128)}, f32[5,4,16,256]{3,2,1,0:T(8,128)S(1)}, u32[]{:S(2)}, u32[]{:S(2)}) collective-permute-start(f32[5,4,16,256]{3,2,1,0:T(8,128)} %get-tuple-element.520), channel_id=1, source_target_pairs={{0,16},{16,32},{32,48},{48,64},{64,80},{80,96},{96,112},{112,128},... | collective-permute-start | bytes 983048 | tf_op jit(solution)/shard_map/ppermute | solution.py:21
  5.7 480.0 %collective-permute-start.1 = (f32[5,4,16,256]{3,2,1,0:T(8,128)}, f32[5,4,16,256]{3,2,1,0:T(8,128)S(1)}, u32[]{:S(2)}, u32[]{:S(2)}) collective-permute-start(f32[5,4,16,256]{3,2,1,0:T(8,128)} %get-tuple-element.519), channel_id=1, source_target_pairs={{16,0},{32,16},{48,32},{64,48},{80,64},{96,80},{112,96},{128,112},... | collective-permute-start | bytes 983048 | tf_op jit(solution)/shard_map/ppermute | solution.py:23
  489.4 5.7 slice-start
  489.5 5.7 slice-start.1
  489.7 11.6 %collective-permute-start.3 = (f32[5,24,4,256]{3,1,2,0:T(8,128)S(1)}, f32[5,24,4,256]{3,1,2,0:T(8,128)S(1)}, u32[]{:S(2)}, u32[]{:S(2)}) collective-permute-start(f32[5,24,4,256]{3,1,2,0:T(8,128)S(1)} %copy.42), channel_id=1, source_target_pairs={{1,0},{2,1},{3,2},{4,3},{5,4},{6,5},{7,6},{8,7},{9,8},{10,9},{11,1... | collective-permute-start | bytes 1474568 | tf_op jit(solution)/shard_map/ppermute | solution.py:23
  494.6 12.6 %collective-permute-start.2 = (f32[5,24,4,256]{3,1,2,0:T(8,128)S(1)}, f32[5,24,4,256]{3,1,2,0:T(8,128)S(1)}, u32[]{:S(2)}, u32[]{:S(2)}) collective-permute-start(f32[5,24,4,256]{3,1,2,0:T(8,128)S(1)} %copy.41), channel_id=1, source_target_pairs={{0,1},{1,2},{2,3},{3,4},{4,5},{5,6},{6,7},{7,8},{8,9},{9,10},{10,1... | collective-permute-start | bytes 1474568 | tf_op jit(solution)/shard_map/ppermute | solution.py:21
  513.7 9.0 copy-start.26
  515.3 45.3 %copy-start.4 = (f32[1,255]{1,0:T(1,128)S(1)}, f32[1,255]{1,0:T(1,128)}, u32[]{:S(2)}) copy-start(f32[1,255]{1,0:T(1,128)} %get-tuple-element.584) | copy-start | bytes 3064
  515.3 45.4 %copy-start.5 = (f32[1,255]{1,0:T(1,128)S(1)}, f32[1,255]{1,0:T(1,128)}, u32[]{:S(2)}) copy-start(f32[1,255]{1,0:T(1,128)} %get-tuple-element.585) | copy-start | bytes 3064
  515.3 45.4 %copy-start.6 = (f32[1,255]{1,0:T(1,128)S(1)}, f32[1,255]{1,0:T(1,128)}, u32[]{:S(2)}) copy-start(f32[1,255]{1,0:T(1,128)} %get-tuple-element.586) | copy-start | bytes 3064
  515.3 45.4 %copy-start.7 = (f32[1,255]{1,0:T(1,128)S(1)}, f32[1,255]{1,0:T(1,128)}, u32[]{:S(2)}) copy-start(f32[1,255]{1,0:T(1,128)} %get-tuple-element.557) | copy-start | bytes 3064
  515.4 45.4 %copy-start.8 = (f32[1,255]{1,0:T(1,128)S(1)}, f32[1,255]{1,0:T(1,128)}, u32[]{:S(2)}) copy-start(f32[1,255]{1,0:T(1,128)} %get-tuple-element.558) | copy-start | bytes 3064
  515.4 45.4 %copy-start.9 = (f32[1,255]{1,0:T(1,128)S(1)}, f32[1,255]{1,0:T(1,128)}, u32[]{:S(2)}) copy-start(f32[1,255]{1,0:T(1,128)} %get-tuple-element.559) | copy-start | bytes 3064
  515.4 45.4 %copy-start.10 = (f32[1,255]{1,0:T(1,128)S(1)}, f32[1,255]{1,0:T(1,128)}, u32[]{:S(2)}) copy-start(f32[1,255]{1,0:T(1,128)} %get-tuple-element.560) | copy-start | bytes 3064
  515.4 45.4 %copy-start.11 = (f32[1,255]{1,0:T(1,128)S(1)}, f32[1,255]{1,0:T(1,128)}, u32[]{:S(2)}) copy-start(f32[1,255]{1,0:T(1,128)} %get-tuple-element.561) | copy-start | bytes 3064
  515.4 45.4 %copy-start.12 = (f32[1,255]{1,0:T(1,128)S(1)}, f32[1,255]{1,0:T(1,128)}, u32[]{:S(2)}) copy-start(f32[1,255]{1,0:T(1,128)} %get-tuple-element.562) | copy-start | bytes 3064
  515.4 45.4 %copy-start.13 = (f32[1,255]{1,0:T(1,128)S(1)}, f32[1,255]{1,0:T(1,128)}, u32[]{:S(2)}) copy-start(f32[1,255]{1,0:T(1,128)} %get-tuple-element.563) | copy-start | bytes 3064
  515.4 45.4 %copy-start.14 = (f32[1,255]{1,0:T(1,128)S(1)}, f32[1,255]{1,0:T(1,128)}, u32[]{:S(2)}) copy-start(f32[1,255]{1,0:T(1,128)} %get-tuple-element.564) | copy-start | bytes 3064
  515.4 45.4 %copy-start.15 = (f32[1,255]{1,0:T(1,128)S(1)}, f32[1,255]{1,0:T(1,128)}, u32[]{:S(2)}) copy-start(f32[1,255]{1,0:T(1,128)} %get-tuple-element.565) | copy-start | bytes 3064
  515.4 45.4 %copy-start.16 = (f32[1,255]{1,0:T(1,128)S(1)}, f32[1,255]{1,0:T(1,128)}, u32[]{:S(2)}) copy-start(f32[1,255]{1,0:T(1,128)} %get-tuple-element.566) | copy-start | bytes 3064
  515.4 45.4 %copy-start.17 = (f32[1,255]{1,0:T(1,128)S(1)}, f32[1,255]{1,0:T(1,128)}, u32[]{:S(2)}) copy-start(f32[1,255]{1,0:T(1,128)} %get-tuple-element.567) | copy-start | bytes 3064
  515.5 45.4 %copy-start.18 = (f32[1,255]{1,0:T(1,128)S(1)}, f32[1,255]{1,0:T(1,128)}, u32[]{:S(2)}) copy-start(f32[1,255]{1,0:T(1,128)} %get-tuple-element.568) | copy-start | bytes 3064
  515.5 45.4 %copy-start.19 = (f32[1,255]{1,0:T(1,128)S(1)}, f32[1,255]{1,0:T(1,128)}, u32[]{:S(2)}) copy-start(f32[1,255]{1,0:T(1,128)} %get-tuple-element.569) | copy-start | bytes 3064
  515.5 45.4 %copy-start.20 = (f32[1,255]{1,0:T(1,128)S(1)}, f32[1,255]{1,0:T(1,128)}, u32[]{:S(2)}) copy-start(f32[1,255]{1,0:T(1,128)} %get-tuple-element.570) | copy-start | bytes 3064
  515.5 45.4 %copy-start.21 = (f32[1,255]{1,0:T(1,128)S(1)}, f32[1,255]{1,0:T(1,128)}, u32[]{:S(2)}) copy-start(f32[1,255]{1,0:T(1,128)} %get-tuple-element.571) | copy-start | bytes 3064
  515.5 45.4 %copy-start.22 = (f32[1,255]{1,0:T(1,128)S(1)}, f32[1,255]{1,0:T(1,128)}, u32[]{:S(2)}) copy-start(f32[1,255]{1,0:T(1,128)} %get-tuple-element.572) | copy-start | bytes 3064
  515.5 45.4 %copy-start.23 = (f32[1,255]{1,0:T(1,128)S(1)}, f32[1,255]{1,0:T(1,128)}, u32[]{:S(2)}) copy-start(f32[1,255]{1,0:T(1,128)} %get-tuple-element.573) | copy-start | bytes 3064
  515.5 45.4 %copy-start.24 = (f32[1,255]{1,0:T(1,128)S(1)}, f32[1,255]{1,0:T(1,128)}, u32[]{:S(2)}) copy-start(f32[1,255]{1,0:T(1,128)} %get-tuple-element.574) | copy-start | bytes 3064
  515.5 45.4 %copy-start.25 = (f32[1,255]{1,0:T(1,128)S(1)}, f32[1,255]{1,0:T(1,128)}, u32[]{:S(2)}) copy-start(f32[1,255]{1,0:T(1,128)} %get-tuple-element.575) | copy-start | bytes 3064
  515.6 66.0 %collective-permute-start.5 = (f32[5,3,16,256]{3,2,1,0:T(8,128)S(1)}, f32[5,3,16,256]{3,2,1,0:T(8,128)S(1)}, u32[]{:S(2)}, u32[]{:S(2)}) collective-permute-start(f32[5,3,16,256]{3,2,1,0:T(8,128)S(1)} %get-tuple-element.518), channel_id=1, source_target_pairs={{0,16},{16,32},{32,48},{48,64},{64,80},{80,96},{96,112},{112,128},... | collective-permute-start | bytes 737288 | tf_op jit(solution)/shard_map/ppermute | solution.py:21
  522.0 59.6 %collective-permute-start.4 = (f32[5,3,16,256]{3,2,1,0:T(8,128)S(1)}, f32[5,3,16,256]{3,2,1,0:T(8,128)}, u32[]{:S(2)}, u32[]{:S(2)}) collective-permute-start(f32[5,3,16,256]{3,2,1,0:T(8,128)S(1)} %get-tuple-element.517), channel_id=1, source_target_pairs={{16,0},{32,16},{48,32},{64,48},{80,64},{96,80},{112,96},{128,112},... | collective-permute-start | bytes 737288 | tf_op jit(solution)/shard_map/ppermute | solution.py:23
  597.4 198.3 %all-to-all-start = ((f32[16,1,20480]{2,1,0:T(1,128)}), f32[16,1,20480]{2,1,0:T(1,128)S(1)}, u32[]{:S(2)}, u32[]{:S(2)}) async-start(f32[16,1,20480]{2,1,0:T(1,128)} %reshape.451), calls=%async_computation | async-start | bytes 2621440 | tf_op jit(solution)/shard_map/all_to_all | solution.py:151
  (6 other events, 12.6 us)
where the time goes:
time: 937 us; the launch traced here: 920 us
  other arithmetic  340 us (36%)
  loops' own time  287 us (31%)
  local copies, waits for them, and re-layouts  178 us (19%)
  between operations  41.6 us (4%)
  blocking collectives  41.3 us (4%)
  starting transfers between devices  24.3 us (3%)
    another operation x2, loops' own time, line_solve(): lax.linalg.tridiagonal_solve(lower, middle, upper, jnp.eye(inner, dtype=j...  287 us
    div x8, other arithmetic, line_solve(): lax.linalg.tridiagonal_solve(lower, middle, upper, jnp.eye(inner, dtype=j...  160 us
    sub x8, other arithmetic, line_solve(): lax.linalg.tridiagonal_solve(lower, middle, upper, jnp.eye(inner, dtype=j...  158 us
    slice x85, local copies, waits for them, and re-layouts, line_solve(): lax.linalg.tridiagonal_solve(lower, middle, upper, jnp.eye(inner, dtype=j...  68.1 us
    all_to_all x1, blocking collectives, body(): lax.all_to_all(solved, 'gx', split_axis=1, concat_axis=3, tiled=True)  41.3 us
    unnamed x62, local copies, waits for them, and re-layouts  33.2 us
    all_to_all x2, local copies, waits for them, and re-layouts, body(): lax.all_to_all(solved, 'gx', split_axis=1, concat_axis=3, tiled=True)  22.1 us
    all_to_all x3, local copies, waits for them, and re-layouts, body(): lax.all_to_all(rhs, 'gx', split_axis=3, concat_axis=1, tiled=True)  20.6 us
  transfers between devices with their start and end apart: 7, of which 2 were waited for; matrix products, arithmetic and copies ran while one was open for 44% of the time, Pallas kernels for 0%

commit v1 on v0

v1 whole, which is shorter than its diff:
```python
import math

import jax
import jax.numpy as jnp
from jax import lax
from jax.experimental import pallas as pl
from jax.experimental.pallas import tpu as pltpu
from jax.sharding import PartitionSpec as P

gamma_gas = 1.4
central_weights = (4.0 / 5.0, -1.0 / 5.0, 4.0 / 105.0, -1.0 / 280.0)
filter_alpha = 0.49
register_decay = -5.0 / 9.0
register_gain = 15.0 / 16.0
time_step = 0.2

ROOT = (-1.0 + math.sqrt(1.0 - 4.0 * filter_alpha**2)) / (2.0 * filter_alpha)
GREEN = 1.0 / math.sqrt(1.0 - 4.0 * filter_alpha**2)
TAPS = (
    (11.0 + 10.0 * filter_alpha) / 16.0,
    (15.0 + 34.0 * filter_alpha) / 64.0,
    (-3.0 + 6.0 * filter_alpha) / 32.0,
    (1.0 - 2.0 * filter_alpha) / 64.0,
)
KAPPA = GREEN * sum(TAPS[abs(n)] * ROOT**n for n in range(-3, 4))
DELTA = tuple(
    GREEN * sum(TAPS[abs(n)] * ROOT ** abs(d - n) for n in range(-3, 4)) - KAPPA * ROOT**d
    for d in range(3)
)

VMEM = pl.BlockSpec(memory_space=pltpu.VMEM)
SMEM = pl.BlockSpec(memory_space=pltpu.SMEM)
F32 = jnp.float32


def primitives(fields):
    density, mom_x, mom_y, mom_z, energy = fields
    inverse = 1.0 / density
    speed_x, speed_y, speed_z = mom_x * inverse, mom_y * inverse, mom_z * inverse
    kinetic = 0.5 * (mom_x * speed_x + mom_y * speed_y + mom_z * speed_z)
    pressure = (gamma_gas - 1.0) * (energy - kinetic)
    return (density, speed_x, speed_y, speed_z, pressure, (energy + pressure) * inverse)


def pair_flux(left, right, direction, weight):
    density, speed_x, speed_y, speed_z, pressure, enthalpy = [a + b for a, b in zip(left, right)]
    normal = (speed_x, speed_y, speed_z)[direction]
    mass = (density * normal) * (0.25 * weight)
    moment = [mass * speed_x, mass * speed_y, mass * speed_z]
    moment[direction] = moment[direction] + pressure * weight
    return [mass + mass] + moment + [mass * enthalpy]


def rows_of(shape, dim):
    return lax.broadcasted_iota(jnp.int32, shape, dim)


def inner_kernel(state_ref, acc_ref, prim_ref):
    @pl.loop(0, 16)
    def _(x):
        for half in range(2):
            rows = pl.ds(8 * half, 8)
            for f, value in enumerate(primitives([state_ref[f, x, rows, :] for f in range(5)])):
                prim_ref[f, x, rows, :] = value

    @pl.loop(0, 16)
    def _(x):
        for half in range(2):
            rows = pl.ds(8 * half, 8)
            own = [prim_ref[f, x, rows, :] for f in range(6)]
            total = [jnp.zeros((8, 256), F32)] * 5
            for l in range(1, 5):
                ahead = [pltpu.roll(value, 256 - l, 1) for value in own]
                flux = pair_flux(own, ahead, 2, central_weights[l - 1])
                total = [part + (pltpu.roll(value, l, 1) - value) for part, value in zip(total, flux)]
            for f in range(5):
                acc_ref[f, x, rows, :] = total[f]

    row = rows_of((16, 128), 0)

    @pl.loop(0, 16)
    def _(x):
        for half in range(2):
            lanes = pl.ds(128 * half, 128)
            own = [prim_ref[f, x, :, lanes] for f in range(6)]
            total = [acc_ref[f, x, :, lanes] for f in range(5)]
            for l in range(1, 5):
                ahead = [pltpu.roll(value, 16 - l, 0) for value in own]
                weight = jnp.where(row < 16 - l, F32(central_weights[l - 1]), F32(0.0))
                flux = pair_flux(own, ahead, 1, weight)
                total = [part + (pltpu.roll(value, l, 0) - value) for part, value in zip(total, flux)]
            for f in range(5):
                acc_ref[f, x, :, lanes] = total[f]

    for half in range(2):
        lanes = pl.ds(128 * half, 128)

        @pl.loop(0, 2)
        def _(tile):
            rows = pl.ds(pl.multiple_of(8 * tile, 8), 8)
            for x in range(16):
                own = [prim_ref[f, x, rows, lanes] for f in range(6)]
                total = [acc_ref[f, x, rows, lanes] for f in range(5)]
                for l in range(1, min(5, 16 - x)):
                    ahead = [prim_ref[f, x + l, rows, lanes] for f in range(6)]
                    flux = pair_flux(own, ahead, 0, central_weights[l - 1])
                    for f in range(5):
                        total[f] = total[f] - flux[f]
                        acc_ref[f, x + l, rows, lanes] = acc_ref[f, x + l, rows, lanes] + flux[f]
                for f in range(5):
                    acc_ref[f, x, rows, lanes] = total[f]


def edge_kernel(
    even_ref, state_ref, register_ref, part_ref, xa_ref, xb_ref, ya_ref, yb_ref,
    out_ref, section_ref, moment_ref, acc_ref, prim_ref, far_ref,
):
    even = even_ref[0] == 1
    row = rows_of((8, 128), 0)

    @pl.loop(0, 16)
    def _(x):
        for half in range(2):
            lanes = pl.ds(128 * half, 128)
            left, right = [], []
            for f in range(5):
                a, b = ya_ref[f, x, :, lanes], yb_ref[f, x, :, lanes]
                below, above = jnp.where(even, a, b), jnp.where(even, b, a)
                left.append(jnp.concatenate([below, state_ref[f, x, 12:16, lanes]], axis=0))
                right.append(jnp.concatenate([state_ref[f, x, 0:4, lanes], above], axis=0))
            left, right = primitives(left), primitives(right)
            low = [jnp.zeros((8, 128), F32)] * 5
            high = [jnp.zeros((8, 128), F32)] * 5
            for l in range(1, 5):
                weight = jnp.where(lax.rem(row, 4) >= 4 - l, F32(central_weights[l - 1]), F32(0.0))
                other = right if l == 4 else [pltpu.roll(value, 4 - l, 0) for value in right]
                flux = pair_flux(left, other, 1, weight)
                high = [part - value for part, value in zip(high, flux)]
                back = flux if l == 4 else [pltpu.roll(value, 4 + l, 0) for value in flux]
                low = [part + value for part, value in zip(low, back)]
            for f in range(5):
                acc_ref[f, x, 0:8, lanes] = part_ref[f, x, 0:8, lanes] + jnp.where(row < 4, low[f], 0.0)
                acc_ref[f, x, 8:16, lanes] = part_ref[f, x, 8:16, lanes] + jnp.where(row >= 4, high[f], 0.0)

    @pl.loop(0, 4)
    def _(x):
        for tile in range(2):
            rows = pl.ds(8 * tile, 8)
            a = [xa_ref[f, x, rows, :] for f in range(5)]
            b = [xb_ref[f, x, rows, :] for f in range(5)]
            before = primitives([jnp.where(even, v, u) for u, v in zip(a, b)])
            after = primitives([jnp.where(even, u, v) for u, v in zip(a, b)])
            first = primitives([state_ref[f, x, rows, :] for f in range(5)])
            last = primitives([state_ref[f, x + 12, rows, :] for f in range(5)])
            for f in range(6):
                far_ref[0, f, x, rows, :] = before[f]
                far_ref[1, f, x, rows, :] = after[f]
                prim_ref[0, f, x, rows, :] = first[f]
                prim_ref[1, f, x, rows, :] = last[f]

    for half in range(2):
        lanes = pl.ds(128 * half, 128)

        @pl.loop(0, 2)
        def _(tile):
            rows = pl.ds(pl.multiple_of(8 * tile, 8), 8)
            for x in range(4):
                own = [prim_ref[0, f, x, rows, lanes] for f in range(6)]
                total = [acc_ref[f, x, rows, lanes] for f in range(5)]
                for l in range(x + 1, 5):
                    left = [far_ref[0, f, 4 + x - l, rows, lanes] for f in range(6)]
                    flux = pair_flux(left, own, 0, central_weights[l - 1])
                    total = [part + value for part, value in zip(total, flux)]
                for f in range(5):
                    acc_ref[f, x, rows, lanes] = total[f]
            for x in range(4):
                own = [prim_ref[1, f, x, rows, lanes] for f in range(6)]
                total = [acc_ref[f, x + 12, rows, lanes] for f in range(5)]
                for l in range(4 - x, 5):
                    right = [far_ref[1, f, x + l - 4, rows, lanes] for f in range(6)]
                    flux = pair_flux(own, right, 0, central_weights[l - 1])
                    total = [part - value for part, value in zip(total, flux)]
                for f in range(5):
                    acc_ref[f, x + 12, rows, lanes] = total[f]

    @pl.loop(0, 5)
    def _(f):
        for tile in range(2):
            rows = pl.ds(8 * tile, 8)
            forward = jnp.zeros((8, 256), F32)
            backward = jnp.zeros((8, 256), F32)
            for x in range(16):
                value = register_decay * register_ref[f, x, rows, :] + time_step * acc_ref[f, x, rows, :]
                out_ref[f, x, rows, :] = value
                value = state_ref[f, x, rows, :] + register_gain * value
                section_ref[f, x, rows, :] = value
                forward = value + ROOT * forward
                backward = backward + ROOT**x * value
            for pair in range(4):
                for half in range(2):
                    q = 2 * (4 * tile + pair) + half
                    lanes = slice(128 * half, 128 * half + 128)
                    moment_ref[q, 0, f] = forward[2 * pair : 2 * pair + 2, lanes]
                    moment_ref[q, 1, f] = backward[2 * pair : 2 * pair + 2, lanes]


def ring_kernel(moment_ref, sums_ref):
    decay = ROOT**16
    close = 1.0 / (1.0 - ROOT**256)
    for f in range(5):
        value = jnp.zeros((2, 128), F32)
        for p in range(16):
            value = moment_ref[p, 0, f] + decay * value
        value = value * close
        for p in range(16):
            sums_ref[p, 0, f] = value
            value = moment_ref[p, 0, f] + decay * value
        value = jnp.zeros((2, 128), F32)
        for p in reversed(range(16)):
            value = moment_ref[p, 1, f] + decay * value
        value = value * close
        for p in reversed(range(16)):
            sums_ref[p, 1, f] = value
            value = moment_ref[p, 1, f] + decay * value


def filter_kernel(even_ref, section_ref, sums_ref, xa_ref, xb_ref, out_ref, ends_ref):
    even = even_ref[0] == 1
    for q in range(16):
        rows = pl.ds(2 * (q // 2), 2)
        lanes = pl.ds(128 * (q % 2), 128)
        for f in range(5):
            ends_ref[0, f, rows, lanes] = sums_ref[q, 0, f]
            ends_ref[1, f, rows, lanes] = sums_ref[q, 1, f]

    @pl.loop(0, 5)
    def _(f):
        for tile in range(2):
            for half in range(2):
                rows, lanes = pl.ds(8 * tile, 8), pl.ds(128 * half, 128)
                a = [xa_ref[f, k, rows, lanes] for k in range(2)]
                b = [xb_ref[f, k, rows, lanes] for k in range(2)]
                cells = [jnp.where(even, v, u) for u, v in zip(a, b)]
                cells += [section_ref[f, x, rows, lanes] for x in range(16)]
                cells += [jnp.where(even, u, v) for u, v in zip(a, b)]
                value = ends_ref[0, f, rows, lanes]
                forward = []
                for x in range(16):
                    value = cells[x + 2] + ROOT * value
                    forward.append(value)
                value = ends_ref[1, f, rows, lanes]
                for x in reversed(range(16)):
                    value = cells[x + 2] + ROOT * value
                    out_ref[f, x, rows, lanes] = (
                        KAPPA * (forward[x] + value)
                        + (DELTA[0] - KAPPA) * cells[x + 2]
                        + DELTA[1] * (cells[x + 1] + cells[x + 3])
                        + DELTA[2] * (cells[x] + cells[x + 4])
                    )


def permutation(step_x, step_y):
    pairs = []
    for g in range(16):
        sign = 1 if g % 2 == 0 else -1
        for y in range(16):
            target = (g + sign * step_x) % 16 * 16 + (y + sign * step_y) % 16
            pairs.append((g * 16 + y, target))
    return pairs


def body(state, register):
    axes = ("gx", "yz")
    shape = (5, 16, 16, 256)
    even = lax.rem(lax.axis_index("gx"), 2) == 0
    even_flag = jnp.reshape(even.astype(jnp.int32), (1,))
    block = jax.ShapeDtypeStruct(shape, F32)
    lines = jax.ShapeDtypeStruct((16, 2, 5, 2, 128), F32)

    y_high, y_low = state[:, :, 12:16], state[:, :, 0:4]
    x_high, x_low = state[:, 12:16], state[:, 0:4]
    ya = lax.ppermute(jnp.where(even, y_high, y_low), axes, permutation(0, 1))
    yb = lax.ppermute(jnp.where(even, y_low, y_high), axes, permutation(0, -1))
    xa = lax.ppermute(jnp.where(even, x_high, x_low), axes, permutation(1, 0))
    xb = lax.ppermute(jnp.where(even, x_low, x_high), axes, permutation(-1, 0))

    part = pl.pallas_call(
        inner_kernel,
        out_shape=block,
        in_specs=[VMEM],
        out_specs=VMEM,
        scratch_shapes=[pltpu.VMEM((6, 16, 16, 256), F32)],
        name="inner",
    )(state)

    register_out, section, moments = pl.pallas_call(
        edge_kernel,
        out_shape=(block, block, lines),
        in_specs=[SMEM] + [VMEM] * 7,
        out_specs=(VMEM, VMEM, VMEM),
        scratch_shapes=[
            pltpu.VMEM(shape, F32),
            pltpu.VMEM((2, 6, 4, 16, 256), F32),
            pltpu.VMEM((2, 6, 4, 16, 256), F32),
        ],
        name="edge",
    )(even_flag, state, register, part, xa, xb, ya, yb)

    s_high, s_low = section[:, 14:16], section[:, 0:2]
    sa = lax.ppermute(jnp.where(even, s_high, s_low), axes, permutation(1, 0))
    sb = lax.ppermute(jnp.where(even, s_low, s_high), axes, permutation(-1, 0))

    moments = lax.all_to_all(moments, "gx", 0, 0, tiled=True)
    sums = pl.pallas_call(
        ring_kernel, out_shape=lines, in_specs=[VMEM], out_specs=VMEM, name="ring"
    )(moments)
    sums = lax.all_to_all(sums, "gx", 0, 0, tiled=True)

    filtered = pl.pallas_call(
        filter_kernel,
        out_shape=block,
        in_specs=[SMEM] + [VMEM] * 4,
        out_specs=VMEM,
        scratch_shapes=[pltpu.VMEM((2, 5, 16, 256), F32)],
        name="filter",
    )(even_flag, section, sums, sa, sb)
    return (register_out, filtered)


def solution(mesh):
    spec = P(None, "gx", "yz", None)
    return jax.shard_map(
        body, mesh=mesh, in_specs=(spec, spec), out_specs=(spec, spec), check_vma=False
    )
```

time: 937 us -> 66.8 us (0.07); the launches traced: 920 us -> 66.4 us
  other arithmetic: 340 us -> 2.4 us
  loops' own time: 287 us -> 0 us
  local copies, waits for them, and re-layouts: 178 us -> 1.69 us
  between operations: 41.6 us -> 0.73 us
  blocking collectives: 41.3 us -> 14.1 us
  Pallas kernels: 0 us -> 23.5 us
    another operation x2 -> x0, loops' own time: 287 us -> none  [line_solve(): lax.linalg.tridiagonal_solve(lower, middle, upper, jnp.eye(inner, dtype=j...]
    div x10 -> x0, other arithmetic: 160 us -> none  [the longest x8 160 us: line_solve(): lax.linalg.tridiagonal_solve(lower, middle, upper, jnp.eye(inner, dtype=j...]
    sub x10 -> x0, other arithmetic: 159 us -> none  [the longest x8 158 us: line_solve(): lax.linalg.tridiagonal_solve(lower, middle, upper, jnp.eye(inner, dtype=j...]
    slice x164 -> x0, local copies, waits for them, and re-layouts: 76.8 us -> none  [the longest x85 68.1 us: line_solve(): lax.linalg.tridiagonal_solve(lower, middle, upper, jnp.eye(inner, dtype=j...]
    all_to_all x5 -> x0, local copies, waits for them, and re-layouts: 42.7 us -> none  [the longest x2 22.1 us: body(): lax.all_to_all(solved, 'gx', split_axis=1, concat_axis=3, tiled=True)]
    unnamed x62 -> x16, local copies, waits for them, and re-layouts: 33.2 us -> 1.69 us
    all_to_all x1, blocking collectives: 41.3 us -> 14.1 us  [body(): moments = lax.all_to_all(moments, 'gx', 0, 0, tiled=True)]
    pallas_call x0 -> x4, Pallas kernels: none -> 23.5 us  [the longest x1 12.5 us: body(): pl.pallas_call(inner_kernel, out_shape=block, in_specs=[VMEM], out_specs=...]
  transfers between devices with their start and end apart: 7 -> 7, of which waited for: 2 -> 2; matrix products, arithmetic and copies ran while one was open for 44% -> 2% of each run, Pallas kernels for 0% -> 19%
where the time goes in v1:
time: 66.8 us; the launch traced here: 66.4 us
  Pallas kernels  23.5 us (35%)
  starting transfers between devices  18.2 us (27%)
  blocking collectives  14.1 us (21%)
  waiting for transfers between devices  5.83 us (9%)
  other arithmetic  2.4 us (4%)
  local copies, waits for them, and re-layouts  1.69 us (3%)
  between operations  0.73 us (1%)
    all_to_all x1, blocking collectives, body(): moments = lax.all_to_all(moments, 'gx', 0, 0, tiled=True)  14.1 us
    pallas_call x1, Pallas kernels, body(): pl.pallas_call(inner_kernel, out_shape=block, in_specs=[VMEM], out_specs=...  12.5 us
    pallas_call x1, Pallas kernels, body(): pl.pallas_call(edge_kernel, out_shape=(block, block, lines), in_specs=[SM...  5.91 us
    ppermute x1, waiting for transfers between devices, body(): sb = lax.ppermute(jnp.where(even, s_low, s_high), axes, permutation(-1, 0))  3.91 us
    ppermute x1, starting transfers between devices, body(): ya = lax.ppermute(jnp.where(even, y_high, y_low), axes, permutation(0, 1))  3.81 us
    ppermute x1, starting transfers between devices, body(): xa = lax.ppermute(jnp.where(even, x_high, x_low), axes, permutation(1, 0))  3.77 us
    all_to_all x1, starting transfers between devices, body(): sums = lax.all_to_all(sums, 'gx', 0, 0, tiled=True)  3.42 us
    pallas_call x1, Pallas kernels, body(): pl.pallas_call(filter_kernel, out_shape=block, in_specs=[SMEM] + [VMEM] *...  3.32 us
  transfers between devices with their start and end apart: 7, of which 2 were waited for; matrix products, arithmetic and copies ran while one was open for 2% of the time, Pallas kernels for 19%

profile of v1, /device:TPU:1, one launch (start us, length us, event | category | flops | bytes accessed | tf_op | source)
XLA Modules:
  0.0 66.4 jit_solution(11869013990756194900)
XLA Ops:
  0.6 0.0 copy-start
  0.6 1.3 %slice_select_fusion = (f32[5,4,16,256]{3,2,1,0:T(8,128)S(1)}, f32[5,4,16,256]{3,2,1,0:T(8,128)S(1)}) fusion(f32[5,16,16,256]{3,2,1,0:T(8,128)} %state_ref.3, pred[]{:T(512)S(6)} %eq.3), kind=kLoop, calls=%fused_computation | loop fusion | flops 163840 | bytes 1310721 | tf_op jit(solution)/shard_map/jit(_where)/select_n | solution.py:285
  1.9 3.1 %collective-permute-start.1 = (f32[5,4,16,256]{3,2,1,0:T(8,128)S(1)}, f32[5,4,16,256]{3,2,1,0:T(8,128)S(1)}, u32[]{:S(2)}, u32[]{:S(2)}) collective-permute-start(f32[5,4,16,256]{3,2,1,0:T(8,128)S(1)} %get-tuple-element.12), channel_id=1, source_target_pairs={{0,240},{1,241},{2,242},{3,243},{4,244},{5,245},{6,246},{7,247},{8... | collective-permute-start | bytes 983048 | tf_op jit(solution)/shard_map/ppermute | solution.py:285
  5.0 3.8 %collective-permute-start = (f32[5,4,16,256]{3,2,1,0:T(8,128)S(1)}, f32[5,4,16,256]{3,2,1,0:T(8,128)S(1)}, u32[]{:S(2)}, u32[]{:S(2)}) collective-permute-start(f32[5,4,16,256]{3,2,1,0:T(8,128)S(1)} %get-tuple-element.13), channel_id=1, source_target_pairs={{0,16},{1,17},{2,18},{3,19},{4,20},{5,21},{6,22},{7,23},{8,24},{9,... | collective-permute-start | bytes 983048 | tf_op jit(solution)/shard_map/ppermute | solution.py:284
  8.8 0.0 copy-done
  8.8 0.1 slice_select_fusion.2
  8.9 1.3 %collective-permute-start.3 = (f32[5,16,4,256]{3,2,1,0:T(4,128)S(1)}, f32[5,16,4,256]{3,2,1,0:T(4,128)S(1)}, u32[]{:S(2)}, u32[]{:S(2)}) collective-permute-start(f32[5,16,4,256]{3,2,1,0:T(4,128)S(1)} %get-tuple-element.10), channel_id=1, source_target_pairs={{0,15},{1,0},{2,1},{3,2},{4,3},{5,4},{6,5},{7,6},{8,7},{9,8},{10,9... | collective-permute-start | bytes 983048 | tf_op jit(solution)/shard_map/ppermute | solution.py:283
  10.2 3.8 %collective-permute-start.2 = (f32[5,16,4,256]{3,2,1,0:T(4,128)S(1)}, f32[5,16,4,256]{3,2,1,0:T(4,128)S(1)}, u32[]{:S(2)}, u32[]{:S(2)}) collective-permute-start(f32[5,16,4,256]{3,2,1,0:T(4,128)S(1)} %get-tuple-element.11), channel_id=1, source_target_pairs={{0,1},{1,2},{2,3},{3,4},{4,5},{5,6},{6,7},{7,8},{8,9},{9,10},{10,1... | collective-permute-start | bytes 983048 | tf_op jit(solution)/shard_map/ppermute | solution.py:282
  14.0 12.5 %inner.1.part_ref = f32[5,16,16,256]{3,2,1,0:T(8,128)} custom-call(f32[5,16,16,256]{3,2,1,0:T(8,128)} %state_ref.3), custom_call_target="tpu_custom_call" | custom-call | tf_op jit(solution)/shard_map/inner/pallas_call | solution.py:287
  26.5 0.0 collective-permute-done.1.xb_ref
  26.5 0.0 collective-permute-done.xa_ref
  26.5 0.0 copy-start.3
  26.6 0.0 collective-permute-done.3.yb_ref
  26.6 0.0 copy-start.4
  26.6 0.0 collective-permute-done.2.ya_ref
  26.6 0.0 copy-start.5
  26.6 0.7 %copy-done.2 = f32[5,4,16,256]{3,2,1,0:T(8,128)} copy-done((f32[5,4,16,256]{3,2,1,0:T(8,128)}, f32[5,4,16,256]{3,2,1,0:T(8,128)S(1)}, u32[]{:S(2)}) %copy-start.2) | copy-done | bytes 327704
  27.3 0.1 copy-done.3
  27.4 0.1 copy-done.4
  27.5 0.1 copy-done.5
  27.6 5.9 %edge.1 = (f32[5,16,16,256]{3,2,1,0:T(8,128)}, f32[5,16,16,256]{3,2,1,0:T(8,128)}, f32[16,2,5,2,128]{4,3,2,1,0:T(2,128)}) custom-call(s32[1]{0:T(128)} %bitcast.even_ref, f32[5,16,16,256]{3,2,1,0:T(8,128)} %state_ref.3, f32[5,16,16,256]{3,2,1,0:T(8,128)} %register_ref.1, f32[5,16,16,256]{3,2,1,0:T(8,128)} %inner.1.part_ref, f32[5,4,16,256]{3,2,1,0:T(8,128)} %copy-done.3, ...), custom_call_target="tpu_custom_call" | custom-call | tf_op jit(solution)/shard_map/edge/pallas_call | solution.py:296
  33.5 14.1 %all_to_all.10.moment_ref = f32[16,2,5,2,128]{4,3,2,1,0:T(2,128)} all-to-all(f32[16,2,5,2,128]{4,3,2,1,0:T(2,128)} %get-tuple-element.7), channel_id=1, replica_groups=mesh['gx'=16,'yz'=16] {'gx'}, dimensions={0} | all-to-all | bytes 327680 | tf_op jit(solution)/shard_map/all_to_all | solution.py:313
  47.6 1.7 %ring.1 = f32[16,2,5,2,128]{4,3,2,1,0:T(2,128)} custom-call(f32[16,2,5,2,128]{4,3,2,1,0:T(2,128)} %all_to_all.10.moment_ref), custom_call_target="tpu_custom_call" | custom-call | tf_op jit(solution)/shard_map/ring/pallas_call | solution.py:314
  49.4 3.4 %all-to-all-start.1 = ((f32[16,2,5,2,128]{4,3,2,1,0:T(2,128)}), f32[16,2,5,2,128]{4,3,2,1,0:T(2,128)S(1)}, u32[]{:S(2)}, u32[]{:S(2)}) async-start(f32[16,2,5,2,128]{4,3,2,1,0:T(2,128)} %ring.1), calls=%async_computation.1 | async-start | bytes 327680 | tf_op jit(solution)/shard_map/all_to_all | solution.py:317
  52.8 1.0 %slice_select_fusion.4 = (f32[5,2,16,256]{3,2,1,0:T(8,128)S(1)}, f32[5,2,16,256]{3,2,1,0:T(8,128)S(1)}) fusion(f32[5,16,16,256]{3,2,1,0:T(8,128)} %get-tuple-element.6.section_ref, pred[]{:T(512)S(6)} %eq.3), kind=kLoop, calls=%fused_computation.4 | loop fusion | flops 81920 | bytes 655361 | tf_op jit(solution)/shard_map/jit(_where)/select_n | solution.py:311
  53.8 1.4 %collective-permute-start.5 = (f32[5,2,16,256]{3,2,1,0:T(8,128)S(1)}, f32[5,2,16,256]{3,2,1,0:T(8,128)S(1)}, u32[]{:S(2)}, u32[]{:S(2)}) collective-permute-start(f32[5,2,16,256]{3,2,1,0:T(8,128)S(1)} %get-tuple-element.8), channel_id=1, source_target_pairs={{0,240},{1,241},{2,242},{3,243},{4,244},{5,245},{6,246},{7,247},{8... | collective-permute-start | bytes 491528 | tf_op jit(solution)/shard_map/ppermute | solution.py:311
  55.2 1.4 %collective-permute-start.4 = (f32[5,2,16,256]{3,2,1,0:T(8,128)S(1)}, f32[5,2,16,256]{3,2,1,0:T(8,128)S(1)}, u32[]{:S(2)}, u32[]{:S(2)}) collective-permute-start(f32[5,2,16,256]{3,2,1,0:T(8,128)S(1)} %get-tuple-element.9), channel_id=1, source_target_pairs={{0,16},{1,17},{2,18},{3,19},{4,20},{5,21},{6,22},{7,23},{8,24},{9,... | collective-permute-start | bytes 491528 | tf_op jit(solution)/shard_map/ppermute | solution.py:310
  56.6 3.9 %collective-permute-done.5.xb_ref = f32[5,2,16,256]{3,2,1,0:T(8,128)S(1)} collective-permute-done((f32[5,2,16,256]{3,2,1,0:T(8,128)S(1)}, f32[5,2,16,256]{3,2,1,0:T(8,128)S(1)}, u32[]{:S(2)}, u32[]{:S(2)}) %collective-permute-start.5) | collective-permute-done | bytes 163872 | tf_op jit(solution)/shard_map/ppermute | solution.py:311
  60.5 0.0 collective-permute-done.4.xa_ref
  60.5 1.9 %all-to-all-done.1.sums_ref = f32[16,2,5,2,128]{4,3,2,1,0:T(2,128)S(1)} async-done(((f32[16,2,5,2,128]{4,3,2,1,0:T(2,128)}), f32[16,2,5,2,128]{4,3,2,1,0:T(2,128)S(1)}, u32[]{:S(2)}, u32[]{:S(2)}) %all-to-all-start.1) | async-done | bytes 163872 | tf_op jit(solution)/shard_map/all_to_all | solution.py:317
  62.4 0.7 copy-done.1
  63.1 3.3 %filter.1 = f32[5,16,16,256]{3,2,1,0:T(8,128)} custom-call(s32[1]{0:T(128)} %bitcast.even_ref, f32[5,16,16,256]{3,2,1,0:T(8,128)} %get-tuple-element.6.section_ref, f32[16,2,5,2,128]{4,3,2,1,0:T(2,128)} %copy-done.1, f32[5,2,16,256]{3,2,1,0:T(8,128)} %copy-done.7, f32[5,2,16,256]{3,2,1,0:T(8,128)} %copy-done.6), custom_call_target="tpu_custom_call" | custom-call | tf_op jit(solution)/shard_map/filter/pallas_call | solution.py:319
  (6 shorter events, 0.0 us)
Async XLA Ops:
  0.6 8.2 %copy-start = (f32[5,16,16,256]{3,2,1,0:T(8,128)S(1)}, f32[5,16,16,256]{3,2,1,0:T(8,128)}, u32[]{:S(2)}) copy-start(f32[5,16,16,256]{3,2,1,0:T(8,128)} %state_ref.3) | copy-start | bytes 3932164
  1.9 24.6 %collective-permute-start.1 = (f32[5,4,16,256]{3,2,1,0:T(8,128)S(1)}, f32[5,4,16,256]{3,2,1,0:T(8,128)S(1)}, u32[]{:S(2)}, u32[]{:S(2)}) collective-permute-start(f32[5,4,16,256]{3,2,1,0:T(8,128)S(1)} %get-tuple-element.12), channel_id=1, source_target_pairs={{0,240},{1,241},{2,242},{3,243},{4,244},{5,245},{6,246},{7,247},{8... | collective-permute-start | bytes 983048 | tf_op jit(solution)/shard_map/ppermute | solution.py:285
  5.0 21.5 %collective-permute-start = (f32[5,4,16,256]{3,2,1,0:T(8,128)S(1)}, f32[5,4,16,256]{3,2,1,0:T(8,128)S(1)}, u32[]{:S(2)}, u32[]{:S(2)}) collective-permute-start(f32[5,4,16,256]{3,2,1,0:T(8,128)S(1)} %get-tuple-element.13), channel_id=1, source_target_pairs={{0,16},{1,17},{2,18},{3,19},{4,20},{5,21},{6,22},{7,23},{8,24},{9,... | collective-permute-start | bytes 983048 | tf_op jit(solution)/shard_map/ppermute | solution.py:284
  8.9 17.6 %collective-permute-start.3 = (f32[5,16,4,256]{3,2,1,0:T(4,128)S(1)}, f32[5,16,4,256]{3,2,1,0:T(4,128)S(1)}, u32[]{:S(2)}, u32[]{:S(2)}) collective-permute-start(f32[5,16,4,256]{3,2,1,0:T(4,128)S(1)} %get-tuple-element.10), channel_id=1, source_target_pairs={{0,15},{1,0},{2,1},{3,2},{4,3},{5,4},{6,5},{7,6},{8,7},{9,8},{10,9... | collective-permute-start | bytes 983048 | tf_op jit(solution)/shard_map/ppermute | solution.py:283
  10.2 16.4 %collective-permute-start.2 = (f32[5,16,4,256]{3,2,1,0:T(4,128)S(1)}, f32[5,16,4,256]{3,2,1,0:T(4,128)S(1)}, u32[]{:S(2)}, u32[]{:S(2)}) collective-permute-start(f32[5,16,4,256]{3,2,1,0:T(4,128)S(1)} %get-tuple-element.11), channel_id=1, source_target_pairs={{0,1},{1,2},{2,3},{3,4},{4,5},{5,6},{6,7},{7,8},{8,9},{9,10},{10,1... | collective-permute-start | bytes 983048 | tf_op jit(solution)/shard_map/ppermute | solution.py:282
  26.5 0.7 %copy-start.2 = (f32[5,4,16,256]{3,2,1,0:T(8,128)}, f32[5,4,16,256]{3,2,1,0:T(8,128)S(1)}, u32[]{:S(2)}) copy-start(f32[5,4,16,256]{3,2,1,0:T(8,128)S(1)} %collective-permute-done.1.xb_ref) | copy-start | bytes 983044
  26.5 0.8 %copy-start.3 = (f32[5,4,16,256]{3,2,1,0:T(8,128)}, f32[5,4,16,256]{3,2,1,0:T(8,128)S(1)}, u32[]{:S(2)}) copy-start(f32[5,4,16,256]{3,2,1,0:T(8,128)S(1)} %collective-permute-done.xa_ref) | copy-start | bytes 983044
  26.6 0.9 %copy-start.4 = (f32[5,16,4,256]{3,2,1,0:T(4,128)}, f32[5,16,4,256]{3,2,1,0:T(4,128)S(1)}, u32[]{:S(2)}) copy-start(f32[5,16,4,256]{3,2,1,0:T(4,128)S(1)} %collective-permute-done.3.yb_ref) | copy-start | bytes 983044
  26.6 1.0 %copy-start.5 = (f32[5,16,4,256]{3,2,1,0:T(4,128)}, f32[5,16,4,256]{3,2,1,0:T(4,128)S(1)}, u32[]{:S(2)}) copy-start(f32[5,16,4,256]{3,2,1,0:T(4,128)S(1)} %collective-permute-done.2.ya_ref) | copy-start | bytes 983044
  49.4 13.1 %all-to-all-start.1 = ((f32[16,2,5,2,128]{4,3,2,1,0:T(2,128)}), f32[16,2,5,2,128]{4,3,2,1,0:T(2,128)S(1)}, u32[]{:S(2)}, u32[]{:S(2)}) async-start(f32[16,2,5,2,128]{4,3,2,1,0:T(2,128)} %ring.1), calls=%async_computation.1 | async-start | bytes 327680 | tf_op jit(solution)/shard_map/all_to_all | solution.py:317
  53.8 6.7 %collective-permute-start.5 = (f32[5,2,16,256]{3,2,1,0:T(8,128)S(1)}, f32[5,2,16,256]{3,2,1,0:T(8,128)S(1)}, u32[]{:S(2)}, u32[]{:S(2)}) collective-permute-start(f32[5,2,16,256]{3,2,1,0:T(8,128)S(1)} %get-tuple-element.8), channel_id=1, source_target_pairs={{0,240},{1,241},{2,242},{3,243},{4,244},{5,245},{6,246},{7,247},{8... | collective-permute-start | bytes 491528 | tf_op jit(solution)/shard_map/ppermute | solution.py:311
  55.2 5.3 %collective-permute-start.4 = (f32[5,2,16,256]{3,2,1,0:T(8,128)S(1)}, f32[5,2,16,256]{3,2,1,0:T(8,128)S(1)}, u32[]{:S(2)}, u32[]{:S(2)}) collective-permute-start(f32[5,2,16,256]{3,2,1,0:T(8,128)S(1)} %get-tuple-element.9), channel_id=1, source_target_pairs={{0,16},{1,17},{2,18},{3,19},{4,20},{5,21},{6,22},{7,23},{8,24},{9,... | collective-permute-start | bytes 491528 | tf_op jit(solution)/shard_map/ppermute | solution.py:310
  60.5 1.9 %copy-start.6 = (f32[5,2,16,256]{3,2,1,0:T(8,128)}, f32[5,2,16,256]{3,2,1,0:T(8,128)S(1)}, u32[]{:S(2)}) copy-start(f32[5,2,16,256]{3,2,1,0:T(8,128)S(1)} %collective-permute-done.5.xb_ref) | copy-start | bytes 491524
  60.5 1.9 %copy-start.7 = (f32[5,2,16,256]{3,2,1,0:T(8,128)}, f32[5,2,16,256]{3,2,1,0:T(8,128)S(1)}, u32[]{:S(2)}) copy-start(f32[5,2,16,256]{3,2,1,0:T(8,128)S(1)} %collective-permute-done.4.xa_ref) | copy-start | bytes 491524
  62.4 0.7 %copy-start.1 = (f32[16,2,5,2,128]{4,3,2,1,0:T(2,128)}, f32[16,2,5,2,128]{4,3,2,1,0:T(2,128)S(1)}, u32[]{:S(2)}) copy-start(f32[16,2,5,2,128]{4,3,2,1,0:T(2,128)S(1)} %all-to-all-done.1.sums_ref) | copy-start | bytes 491524

commit v2 on v1

v2 whole, which is shorter than its diff:
```python
import math

import jax
import jax.numpy as jnp
from jax import lax
from jax.experimental import pallas as pl
from jax.experimental.pallas import tpu as pltpu
from jax.sharding import PartitionSpec as P

gamma_gas = 1.4
central_weights = (4.0 / 5.0, -1.0 / 5.0, 4.0 / 105.0, -1.0 / 280.0)
filter_alpha = 0.49
register_decay = -5.0 / 9.0
register_gain = 15.0 / 16.0
time_step = 0.2

ROOT = (-1.0 + math.sqrt(1.0 - 4.0 * filter_alpha**2)) / (2.0 * filter_alpha)
GREEN = 1.0 / math.sqrt(1.0 - 4.0 * filter_alpha**2)
TAPS = (
    (11.0 + 10.0 * filter_alpha) / 16.0,
    (15.0 + 34.0 * filter_alpha) / 64.0,
    (-3.0 + 6.0 * filter_alpha) / 32.0,
    (1.0 - 2.0 * filter_alpha) / 64.0,
)
KAPPA = GREEN * sum(TAPS[abs(n)] * ROOT**n for n in range(-3, 4))
DELTA = tuple(
    GREEN * sum(TAPS[abs(n)] * ROOT ** abs(d - n) for n in range(-3, 4)) - KAPPA * ROOT**d
    for d in range(3)
)

VMEM = pl.BlockSpec(memory_space=pltpu.VMEM)
SMEM = pl.BlockSpec(memory_space=pltpu.SMEM)
ANY = pl.BlockSpec(memory_space=pl.ANY)
F32 = jnp.float32
GRANT = pltpu.CompilerParams(vmem_limit_bytes=16 << 20)


def near(value):
    return pltpu.with_memory_space_constraint(value, pltpu.VMEM)


def primitives(fields):
    density, mom_x, mom_y, mom_z, energy = fields
    inverse = 1.0 / density
    speed_x, speed_y, speed_z = mom_x * inverse, mom_y * inverse, mom_z * inverse
    kinetic = 0.5 * (mom_x * speed_x + mom_y * speed_y + mom_z * speed_z)
    pressure = (gamma_gas - 1.0) * (energy - kinetic)
    return (density, speed_x, speed_y, speed_z, pressure, (energy + pressure) * inverse)


def pair_flux(left, right, direction, weight):
    density, speed_x, speed_y, speed_z, pressure, enthalpy = [a + b for a, b in zip(left, right)]
    normal = (speed_x, speed_y, speed_z)[direction]
    mass = (density * normal) * (0.25 * weight)
    moment = [mass * speed_x, mass * speed_y, mass * speed_z]
    moment[direction] = moment[direction] + pressure * weight
    return [mass + mass] + moment + [mass * enthalpy]


def rows_of(shape, dim):
    return lax.broadcasted_iota(jnp.int32, shape, dim)


def pack_kernel(even_ref, state_any, state_ref, ya_ref, yb_ref, xa_ref, xb_ref, sems):
    copies = [pltpu.make_async_copy(state_any.at[f], state_ref.at[f], sems.at[f]) for f in range(5)]
    for copy in copies:
        copy.start()
    even = even_ref[0] == 1
    for f in range(5):
        copies[f].wait()

        @pl.loop(0, 4)
        def _(step):
            for k in range(4):
                x = 4 * step + k
                low, high = state_ref[f, x, 0:4, :], state_ref[f, x, 12:16, :]
                ya_ref[f, x] = jnp.where(even, high, low)
                yb_ref[f, x] = jnp.where(even, low, high)
            xa_ref[f, step] = state_ref[f, jnp.where(even, 12, 0) + step]
            xb_ref[f, step] = state_ref[f, jnp.where(even, 0, 12) + step]


def inner_kernel(state_ref, part_ref, prim_ref):
    row = rows_of((16, 128), 0)
    below = [jnp.where(row < 16 - l, F32(central_weights[l - 1]), F32(0.0)) for l in range(1, 5)]

    @pl.loop(0, 16)
    def _(x):
        prims = [primitives([state_ref[f, x, 8 * half : 8 * half + 8, :] for f in range(5)]) for half in range(2)]
        along = [[None, None] for _ in range(5)]
        for half in range(2):
            own = prims[half]
            for f in range(6):
                prim_ref[f, x, 8 * half : 8 * half + 8, :] = own[f]
            total = [jnp.zeros((8, 256), F32)] * 5
            for l in range(1, 5):
                ahead = [pltpu.roll(value, 256 - l, 1) for value in own]
                flux = pair_flux(own, ahead, 2, central_weights[l - 1])
                total = [part + (pltpu.roll(value, l, 1) - value) for part, value in zip(total, flux)]
            for f in range(5):
                along[f][half] = total[f]
        for half in range(2):
            lanes = pl.ds(128 * half, 128)
            cut = slice(128 * half, 128 * half + 128)
            own = [jnp.concatenate([prims[0][f][:, cut], prims[1][f][:, cut]], axis=0) for f in range(6)]
            total = [jnp.zeros((16, 128), F32)] * 5
            for l in range(1, 5):
                ahead = [pltpu.roll(value, 16 - l, 0) for value in own]
                flux = pair_flux(own, ahead, 1, below[l - 1])
                total = [part + (pltpu.roll(value, l, 0) - value) for part, value in zip(total, flux)]
            for f in range(5):
                part_ref[f, x, :, lanes] = total[f] + jnp.concatenate(
                    [along[f][0][:, cut], along[f][1][:, cut]], axis=0
                )

    for half in range(2):
        lanes = pl.ds(128 * half, 128)

        @pl.loop(0, 2)
        def _(tile):
            rows = pl.ds(pl.multiple_of(8 * tile, 8), 8)
            for x in range(16):
                own = [prim_ref[f, x, rows, lanes] for f in range(6)]
                total = [part_ref[f, x, rows, lanes] for f in range(5)]
                for l in range(1, min(5, 16 - x)):
                    ahead = [prim_ref[f, x + l, rows, lanes] for f in range(6)]
                    flux = pair_flux(own, ahead, 0, central_weights[l - 1])
                    for f in range(5):
                        total[f] = total[f] - flux[f]
                        part_ref[f, x + l, rows, lanes] = part_ref[f, x + l, rows, lanes] + flux[f]
                for f in range(5):
                    part_ref[f, x, rows, lanes] = total[f]


def edge_kernel(
    even_ref, state_ref, part_ref, register_any, xa_any, xb_any, ya_any, yb_any,
    out_any, section_any, moment_ref, sa_ref, sb_ref,
    acc_ref, prim_ref, far_ref, register_ref, xa_ref, xb_ref, ya_ref, yb_ref, out_ref, section_ref,
    in_sems, out_sems,
):
    even = even_ref[0] == 1
    row = rows_of((8, 128), 0)
    arrivals = [
        pltpu.make_async_copy(source, target, in_sems.at[k])
        for k, (source, target) in enumerate(
            ((xa_any, xa_ref), (xb_any, xb_ref), (ya_any, ya_ref), (yb_any, yb_ref), (register_any, register_ref))
        )
    ]
    for copy in arrivals:
        copy.start()
    departures = [
        [
            pltpu.make_async_copy(out_ref.at[f], out_any.at[f], out_sems.at[0, f]),
            pltpu.make_async_copy(section_ref.at[f], section_any.at[f], out_sems.at[1, f]),
        ]
        for f in range(5)
    ]

    @pl.loop(4, 12)
    def _(x):
        for f in range(5):
            acc_ref[f, x] = part_ref[f, x]

    @pl.loop(0, 4)
    def _(x):
        for tile in range(2):
            rows = pl.ds(8 * tile, 8)
            first = primitives([state_ref[f, x, rows, :] for f in range(5)])
            last = primitives([state_ref[f, x + 12, rows, :] for f in range(5)])
            for f in range(6):
                prim_ref[0, f, x, rows, :] = first[f]
                prim_ref[1, f, x, rows, :] = last[f]

    arrivals[0].wait()
    arrivals[1].wait()

    @pl.loop(0, 4)
    def _(x):
        for tile in range(2):
            rows = pl.ds(8 * tile, 8)
            a = [xa_ref[f, x, rows, :] for f in range(5)]
            b = [xb_ref[f, x, rows, :] for f in range(5)]
            before = primitives([jnp.where(even, v, u) for u, v in zip(a, b)])
            after = primitives([jnp.where(even, u, v) for u, v in zip(a, b)])
            for f in range(6):
                far_ref[0, f, x, rows, :] = before[f]
                far_ref[1, f, x, rows, :] = after[f]

    for half in range(2):
        lanes = pl.ds(128 * half, 128)

        @pl.loop(0, 2)
        def _(tile):
            rows = pl.ds(pl.multiple_of(8 * tile, 8), 8)
            for x in range(4):
                own = [prim_ref[0, f, x, rows, lanes] for f in range(6)]
                total = [part_ref[f, x, rows, lanes] for f in range(5)]
                for l in range(x + 1, 5):
                    left = [far_ref[0, f, 4 + x - l, rows, lanes] for f in range(6)]
                    flux = pair_flux(left, own, 0, central_weights[l - 1])
                    total = [part + value for part, value in zip(total, flux)]
                for f in range(5):
                    acc_ref[f, x, rows, lanes] = total[f]
            for x in range(4):
                own = [prim_ref[1, f, x, rows, lanes] for f in range(6)]
                total = [part_ref[f, x + 12, rows, lanes] for f in range(5)]
                for l in range(4 - x, 5):
                    right = [far_ref[1, f, x + l - 4, rows, lanes] for f in range(6)]
                    flux = pair_flux(own, right, 0, central_weights[l - 1])
                    total = [part - value for part, value in zip(total, flux)]
                for f in range(5):
                    acc_ref[f, x + 12, rows, lanes] = total[f]

    arrivals[2].wait()
    arrivals[3].wait()

    @pl.loop(0, 16)
    def _(x):
        for half in range(2):
            lanes = pl.ds(128 * half, 128)
            left, right = [], []
            for f in range(5):
                a, b = ya_ref[f, x, :, lanes], yb_ref[f, x, :, lanes]
                below, above = jnp.where(even, a, b), jnp.where(even, b, a)
                left.append(jnp.concatenate([below, state_ref[f, x, 12:16, lanes]], axis=0))
                right.append(jnp.concatenate([state_ref[f, x, 0:4, lanes], above], axis=0))
            left, right = primitives(left), primitives(right)
            low = [jnp.zeros((8, 128), F32)] * 5
            high = [jnp.zeros((8, 128), F32)] * 5
            for l in range(1, 5):
                weight = jnp.where(lax.rem(row, 4) >= 4 - l, F32(central_weights[l - 1]), F32(0.0))
                other = right if l == 4 else [pltpu.roll(value, 4 - l, 0) for value in right]
                flux = pair_flux(left, other, 1, weight)
                high = [part - value for part, value in zip(high, flux)]
                back = flux if l == 4 else [pltpu.roll(value, 4 + l, 0) for value in flux]
                low = [part + value for part, value in zip(low, back)]
            for f in range(5):
                acc_ref[f, x, 0:8, lanes] = acc_ref[f, x, 0:8, lanes] + jnp.where(row < 4, low[f], 0.0)
                acc_ref[f, x, 8:16, lanes] = acc_ref[f, x, 8:16, lanes] + jnp.where(row >= 4, high[f], 0.0)

    arrivals[4].wait()
    for f in range(5):

        @pl.loop(0, 2)
        def _(tile):
            rows = pl.ds(pl.multiple_of(8 * tile, 8), 8)
            forward = jnp.zeros((8, 256), F32)
            backward = jnp.zeros((8, 256), F32)
            for x in range(16):
                value = register_decay * register_ref[f, x, rows, :] + time_step * acc_ref[f, x, rows, :]
                out_ref[f, x, rows, :] = value
                value = state_ref[f, x, rows, :] + register_gain * value
                section_ref[f, x, rows, :] = value
                forward = value + ROOT * forward
                backward = backward + ROOT**x * value
            for pair in range(4):
                for half in range(2):
                    q = 2 * (4 * tile + pair) + half
                    lanes = slice(128 * half, 128 * half + 128)
                    moment_ref[q, 0, f] = forward[2 * pair : 2 * pair + 2, lanes]
                    moment_ref[q, 1, f] = backward[2 * pair : 2 * pair + 2, lanes]
        for copy in departures[f]:
            copy.start()
        for k in range(2):
            sa_ref[f, k] = section_ref[f, jnp.where(even, 14, 0) + k]
            sb_ref[f, k] = section_ref[f, jnp.where(even, 0, 14) + k]
    for pair in departures:
        for copy in pair:
            copy.wait()


def ring_kernel(moment_ref, local_any, sums_ref):
    decay = ROOT**16
    close = 1.0 / (1.0 - ROOT**256)
    for f in range(5):
        value = jnp.zeros((2, 128), F32)
        for p in range(16):
            value = moment_ref[p, 0, f] + decay * value
        value = value * close
        for p in range(16):
            sums_ref[p, 0, f] = value
            value = moment_ref[p, 0, f] + decay * value
        value = jnp.zeros((2, 128), F32)
        for p in reversed(range(16)):
            value = moment_ref[p, 1, f] + decay * value
        value = value * close
        for p in reversed(range(16)):
            sums_ref[p, 1, f] = value
            value = moment_ref[p, 1, f] + decay * value


def local_kernel(even_ref, section_any, xa_ref, xb_ref, out_ref, section_ref, sems):
    even = even_ref[0] == 1
    arrivals = [pltpu.make_async_copy(section_any.at[f], section_ref.at[f], sems.at[f]) for f in range(5)]
    for copy in arrivals:
        copy.start()
    for f in range(5):
        arrivals[f].wait()

        @pl.loop(0, 2)
        def _(tile):
            for half in range(2):
                rows, lanes = pl.ds(pl.multiple_of(8 * tile, 8), 8), pl.ds(128 * half, 128)
                a = [xa_ref[f, k, rows, lanes] for k in range(2)]
                b = [xb_ref[f, k, rows, lanes] for k in range(2)]
                cells = [jnp.where(even, v, u) for u, v in zip(a, b)]
                cells += [section_ref[f, x, rows, lanes] for x in range(16)]
                cells += [jnp.where(even, u, v) for u, v in zip(a, b)]
                value = cells[2]
                forward = [value]
                for x in range(1, 16):
                    value = cells[x + 2] + ROOT * value
                    forward.append(value)
                value = jnp.zeros((8, 128), F32)
                for x in reversed(range(16)):
                    value = cells[x + 2] + ROOT * value
                    out_ref[f, x, rows, lanes] = (
                        KAPPA * (forward[x] + value)
                        + (DELTA[0] - KAPPA) * cells[x + 2]
                        + DELTA[1] * (cells[x + 1] + cells[x + 3])
                        + DELTA[2] * (cells[x] + cells[x + 4])
                    )


def filter_kernel(local_ref, sums_ref, out_ref, ends_ref, full_ref, sems):
    for q in range(16):
        rows = pl.ds(2 * (q // 2), 2)
        lanes = pl.ds(128 * (q % 2), 128)
        for f in range(5):
            ends_ref[0, f, rows, lanes] = sums_ref[q, 0, f]
            ends_ref[1, f, rows, lanes] = sums_ref[q, 1, f]
    copies = [pltpu.make_async_copy(full_ref.at[f], out_ref.at[f], sems.at[f]) for f in range(5)]
    for f in range(5):

        @pl.loop(0, 2)
        def _(tile):
            rows = pl.ds(pl.multiple_of(8 * tile, 8), 8)
            before, after = ends_ref[0, f, rows, :], ends_ref[1, f, rows, :]
            for x in range(16):
                full_ref[f, x, rows, :] = local_ref[f, x, rows, :] + (
                    KAPPA * ROOT ** (x + 1) * before + KAPPA * ROOT ** (16 - x) * after
                )

        copies[f].start()
    for copy in copies:
        copy.wait()


def permutation(step_x, step_y):
    pairs = []
    for g in range(16):
        sign = 1 if g % 2 == 0 else -1
        for y in range(16):
            target = (g + sign * step_x) % 16 * 16 + (y + sign * step_y) % 16
            pairs.append((g * 16 + y, target))
    return pairs


def body(state, register):
    axes = ("gx", "yz")
    shape = (5, 16, 16, 256)
    even = lax.rem(lax.axis_index("gx"), 2) == 0
    even_flag = jnp.reshape(even.astype(jnp.int32), (1,))
    lines = (16, 2, 5, 2, 128)

    y_send = pltpu.VMEM((5, 16, 4, 256), F32)
    x_send = pltpu.VMEM((5, 4, 16, 256), F32)
    state, ya, yb, xa, xb = pl.pallas_call(
        pack_kernel,
        out_shape=(pltpu.VMEM(shape, F32), y_send, y_send, x_send, x_send),
        in_specs=[SMEM, ANY],
        out_specs=(VMEM,) * 5,
        scratch_shapes=[pltpu.SemaphoreType.DMA((5,))],
        compiler_params=GRANT,
        name="pack",
    )(even_flag, state)
    ya = lax.ppermute(ya, axes, permutation(0, 1))
    yb = lax.ppermute(yb, axes, permutation(0, -1))
    xa = lax.ppermute(xa, axes, permutation(1, 0))
    xb = lax.ppermute(xb, axes, permutation(-1, 0))

    state = near(state)
    part = pl.pallas_call(
        inner_kernel,
        out_shape=pltpu.VMEM(shape, F32),
        in_specs=[VMEM],
        out_specs=VMEM,
        scratch_shapes=[pltpu.VMEM((6, 16, 16, 256), F32)],
        compiler_params=GRANT,
        name="inner",
    )(state)

    block = jax.ShapeDtypeStruct(shape, F32)
    send = pltpu.VMEM((5, 2, 16, 256), F32)
    register_out, section, moments, sa, sb = pl.pallas_call(
        edge_kernel,
        out_shape=(block, block, pltpu.VMEM(lines, F32), send, send),
        in_specs=[SMEM, VMEM, VMEM] + [ANY] * 5,
        out_specs=(ANY, ANY, VMEM, VMEM, VMEM),
        scratch_shapes=[
            pltpu.VMEM(shape, F32),
            pltpu.VMEM((2, 6, 4, 16, 256), F32),
            pltpu.VMEM((2, 6, 4, 16, 256), F32),
            pltpu.VMEM(shape, F32),
            pltpu.VMEM((5, 4, 16, 256), F32),
            pltpu.VMEM((5, 4, 16, 256), F32),
            pltpu.VMEM((5, 16, 4, 256), F32),
            pltpu.VMEM((5, 16, 4, 256), F32),
            pltpu.VMEM(shape, F32),
            pltpu.VMEM(shape, F32),
            pltpu.SemaphoreType.DMA((5,)),
            pltpu.SemaphoreType.DMA((2, 5)),
        ],
        compiler_params=GRANT,
        name="edge",
    )(even_flag, state, near(part), register, xa, xb, ya, yb)

    moments = lax.all_to_all(moments, "gx", 0, 0, tiled=True)
    sa = lax.ppermute(sa, axes, permutation(1, 0))
    sb = lax.ppermute(sb, axes, permutation(-1, 0))
    local = pl.pallas_call(
        local_kernel,
        out_shape=pltpu.VMEM(shape, F32),
        in_specs=[SMEM, ANY, VMEM, VMEM],
        out_specs=VMEM,
        scratch_shapes=[pltpu.VMEM(shape, F32), pltpu.SemaphoreType.DMA((5,))],
        compiler_params=GRANT,
        name="local",
    )(even_flag, section, sa, sb)
    sums = pl.pallas_call(
        ring_kernel,
        out_shape=pltpu.VMEM(lines, F32),
        in_specs=[VMEM, ANY],
        out_specs=VMEM,
        compiler_params=GRANT,
        name="ring",
    )(near(moments), local)
    sums = lax.all_to_all(sums, "gx", 0, 0, tiled=True)

    filtered = pl.pallas_call(
        filter_kernel,
        out_shape=jax.ShapeDtypeStruct(shape, F32),
        in_specs=[VMEM] * 2,
        out_specs=pl.BlockSpec(memory_space=pltpu.HBM),
        scratch_shapes=[
            pltpu.VMEM((2, 5, 16, 256), F32),
            pltpu.VMEM(shape, F32),
            pltpu.SemaphoreType.DMA((5,)),
        ],
        compiler_params=GRANT,
        name="filter",
    )(near(local), near(sums))
    return (register_out, filtered)


def solution(mesh):
    spec = P(None, "gx", "yz", None)
    return jax.shard_map(
        body, mesh=mesh, in_specs=(spec, spec), out_specs=(spec, spec), check_vma=False
    )
```

time: 66.8 us -> 57.7 us (0.86)
  Pallas kernels: 23.5 us -> 13.3 us
  waiting for transfers between devices: 5.83 us -> 13.6 us
  starting transfers between devices: 18.2 us -> 14 us
  other arithmetic: 2.4 us -> 0 us
    pallas_call x4 -> x6, Pallas kernels: 23.5 us -> 13.3 us  [the longest x1 6.5 us: body(): pl.pallas_call(inner_kernel, out_shape=pltpu.VMEM(shape, F32), in_specs=[...]
    ppermute x6, waiting for transfers between devices: 3.93 us -> 12.6 us  [the longest x1 6.31 us: body(): sb = lax.ppermute(sb, axes, permutation(-1, 0))]
    ppermute x6, starting transfers between devices: 14.8 us -> 9.88 us  [the longest x1 4.84 us: body(): ya = lax.ppermute(ya, axes, permutation(0, 1))]
    select_n x3 -> x0, other arithmetic: 2.4 us -> none  [the longest x1 1.25 us: body(): xb = lax.ppermute(jnp.where(even, x_low, x_high), axes, permutation(-1, 0))]
    all_to_all x1, waiting for transfers between devices: 1.9 us -> 1.02 us  [body(): moments = lax.all_to_all(moments, 'gx', 0, 0, tiled=True)]
    all_to_all x1, starting transfers between devices: 3.42 us -> 4.15 us  [body(): moments = lax.all_to_all(moments, 'gx', 0, 0, tiled=True)]
    unnamed x16 -> x4, local copies, waits for them, and re-layouts: 1.69 us -> 1.31 us
  transfers between devices with their start and end apart: 7 -> 7, of which waited for: 2 -> 3; matrix products, arithmetic and copies ran while one was open for 2% -> 0% of each run, Pallas kernels for 19% -> 13%
where the time goes in v2:
time: 57.7 us; the launch traced here: 57.4 us
  blocking collectives  14.5 us (25%)
  starting transfers between devices  14 us (24%)
  waiting for transfers between devices  13.6 us (24%)
  Pallas kernels  13.3 us (23%)
  local copies, waits for them, and re-layouts  1.31 us (2%)
  between operations  0.71 us (1%)
    all_to_all x1, blocking collectives, body(): sums = lax.all_to_all(sums, 'gx', 0, 0, tiled=True)  14.5 us
    pallas_call x1, Pallas kernels, body(): pl.pallas_call(inner_kernel, out_shape=pltpu.VMEM(shape, F32), in_specs=[...  6.5 us
    ppermute x1, waiting for transfers between devices, body(): sb = lax.ppermute(sb, axes, permutation(-1, 0))  6.31 us
    ppermute x1, waiting for transfers between devices, body(): yb = lax.ppermute(yb, axes, permutation(0, -1))  6.25 us
    ppermute x1, starting transfers between devices, body(): ya = lax.ppermute(ya, axes, permutation(0, 1))  4.84 us
    pallas_call x1, Pallas kernels, body(): pl.pallas_call(edge_kernel, out_shape=(block, block, pltpu.VMEM(lines, F3...  4.16 us
    all_to_all x1, starting transfers between devices, body(): moments = lax.all_to_all(moments, 'gx', 0, 0, tiled=True)  4.15 us
    ppermute x1, starting transfers between devices, body(): xa = lax.ppermute(xa, axes, permutation(1, 0))  3.29 us
  transfers between devices with their start and end apart: 7, of which 3 were waited for; matrix products, arithmetic and copies ran while one was open for 0% of the time, Pallas kernels for 13%

profile of v2, /device:TPU:1, one launch (start us, length us, event | category | flops | bytes accessed | tf_op | source)
XLA Modules:
  0.0 57.4 jit_solution(1598694125267691543)
XLA Ops:
  0.6 0.0 copy-start
  0.6 1.3 %copy-done = f32[5,16,16,256]{3,2,1,0:T(8,128)S(1)} copy-done((f32[5,16,16,256]{3,2,1,0:T(8,128)S(1)}, f32[5,16,16,256]{3,2,1,0:T(8,128)}, u32[]{:S(2)}) %copy-start) | copy-done | bytes 1310744
  2.0 0.4 pack.1
  2.3 3.3 %collective-permute-start = (f32[5,4,16,256]{3,2,1,0:T(8,128)S(1)}, f32[5,4,16,256]{3,2,1,0:T(8,128)S(1)}, u32[]{:S(2)}, u32[]{:S(2)}) collective-permute-start(f32[5,4,16,256]{3,2,1,0:T(8,128)S(1)} %get-tuple-element.13), channel_id=1, source_target_pairs={{0,16},{1,17},{2,18},{3,19},{4,20},{5,21},{6,22},{7,23},{8,24},{9,... | collective-permute-start | bytes 983048 | tf_op jit(solution)/shard_map/ppermute | solution.py:379
  5.6 0.0 collective-permute-start.1
  5.6 4.8 %collective-permute-start.2 = (f32[5,16,4,256]{3,2,1,0:T(4,128)S(1)}, f32[5,16,4,256]{3,2,1,0:T(4,128)S(1)}, u32[]{:S(2)}, u32[]{:S(2)}) collective-permute-start(f32[5,16,4,256]{3,2,1,0:T(4,128)S(1)} %get-tuple-element.15), channel_id=1, source_target_pairs={{0,1},{1,2},{2,3},{3,4},{4,5},{5,6},{6,7},{7,8},{8,9},{9,10},{10,1... | collective-permute-start | bytes 983048 | tf_op jit(solution)/shard_map/ppermute | solution.py:377
  10.5 0.0 collective-permute-start.3
  10.5 0.0 copy-start.1
  10.5 6.5 %inner.1.part_ref = f32[5,16,16,256]{3,2,1,0:T(8,128)S(1)} custom-call(f32[5,16,16,256]{3,2,1,0:T(8,128)S(1)} %get-tuple-element.12.state_ref), custom_call_target="tpu_custom_call" | custom-call | tf_op jit(solution)/shard_map/inner/pallas_call | solution.py:383
  17.0 0.0 collective-permute-done.xa_any
  17.0 0.0 collective-permute-done.1.xb_any
  17.0 0.0 collective-permute-done.2.ya_any
  17.0 6.3 %collective-permute-done.3.yb_any = f32[5,16,4,256]{3,2,1,0:T(4,128)S(1)} collective-permute-done((f32[5,16,4,256]{3,2,1,0:T(4,128)S(1)}, f32[5,16,4,256]{3,2,1,0:T(4,128)S(1)}, u32[]{:S(2)}, u32[]{:S(2)}) %collective-permute-start.3) | collective-permute-done | bytes 327712 | tf_op jit(solution)/shard_map/ppermute | solution.py:378
  23.3 0.0 copy-done.1
  23.3 4.2 %edge.1 = (f32[5,16,16,256]{3,2,1,0:T(8,128)}, f32[5,16,16,256]{3,2,1,0:T(8,128)S(1)}, f32[16,2,5,2,128]{4,3,2,1,0:T(2,128)}, f32[5,2,16,256]{3,2,1,0:T(8,128)S(1)}, f32[5,2,16,256]{3,2,1,0:T(8,128)S(1)}) custom-call(s32[1]{0:T(128)} %bitcast.even_ref, f32[5,16,16,256]{3,2,1,0:T(8,128)S(1)} %get-tuple-element.12.state_ref, ...), custom_call_target="tpu_custom_call" | custom-call | tf_op jit(solution)/shard_map/edge/pallas_call | solution.py:395
  27.4 4.1 %all-to-all-start = ((f32[16,2,5,2,128]{4,3,2,1,0:T(2,128)}), f32[16,2,5,2,128]{4,3,2,1,0:T(2,128)S(1)}, u32[]{:S(2)}, u32[]{:S(2)}) async-start(f32[16,2,5,2,128]{4,3,2,1,0:T(2,128)} %get-tuple-element.21), calls=%async_computation | async-start | bytes 327680 | tf_op jit(solution)/shard_map/all_to_all | solution.py:418
  31.6 0.2 collective-permute-start.4
  31.8 1.6 %collective-permute-start.5 = (f32[5,2,16,256]{3,2,1,0:T(8,128)S(1)}, f32[5,2,16,256]{3,2,1,0:T(8,128)S(1)}, u32[]{:S(2)}, u32[]{:S(2)}) collective-permute-start(f32[5,2,16,256]{3,2,1,0:T(8,128)S(1)} %get-tuple-element.20), channel_id=1, source_target_pairs={{0,240},{1,241},{2,242},{3,243},{4,244},{5,245},{6,246},{7,247},{8... | collective-permute-start | bytes 491528 | tf_op jit(solution)/shard_map/ppermute | solution.py:420
  33.3 0.0 collective-permute-done.4.xa_ref
  33.3 6.3 %collective-permute-done.5.xb_ref = f32[5,2,16,256]{3,2,1,0:T(8,128)S(1)} collective-permute-done((f32[5,2,16,256]{3,2,1,0:T(8,128)S(1)}, f32[5,2,16,256]{3,2,1,0:T(8,128)S(1)}, u32[]{:S(2)}, u32[]{:S(2)}) %collective-permute-start.5) | collective-permute-done | bytes 163872 | tf_op jit(solution)/shard_map/ppermute | solution.py:420
  39.7 0.9 %local.1.local_any.local_ref = f32[5,16,16,256]{3,2,1,0:T(8,128)S(1)} custom-call(s32[1]{0:T(128)} %bitcast.even_ref, f32[5,16,16,256]{3,2,1,0:T(8,128)S(1)} %get-tuple-element.18.section_any, f32[5,2,16,256]{3,2,1,0:T(8,128)S(1)} %collective-permute-done.4.xa_ref, f32[5,2,16,256]{3,2,1,0:T(8,128)S(1)} %collective-permute-done.5.xb_ref), custom_call_target="tpu_custom_call" | custom-call | tf_op jit(solution)/shard_map/local/pallas_call | solution.py:421
  40.6 1.0 %all-to-all-done.moment_ref = f32[16,2,5,2,128]{4,3,2,1,0:T(2,128)S(1)} async-done(((f32[16,2,5,2,128]{4,3,2,1,0:T(2,128)}), f32[16,2,5,2,128]{4,3,2,1,0:T(2,128)S(1)}, u32[]{:S(2)}, u32[]{:S(2)}) %all-to-all-start) | async-done | bytes 163872 | tf_op jit(solution)/shard_map/all_to_all | solution.py:418
  41.6 0.2 ring.1
  41.8 14.5 %all_to_all.10.sums_ref = f32[16,2,5,2,128]{4,3,2,1,0:T(2,128)S(1)} all-to-all(f32[16,2,5,2,128]{4,3,2,1,0:T(2,128)S(1)} %ring.1), channel_id=1, replica_groups=mesh['gx'=16,'yz'=16] {'gx'}, dimensions={0} | all-to-all | bytes 327680 | tf_op jit(solution)/shard_map/all_to_all | solution.py:438
  56.2 1.2 %filter.1 = f32[5,16,16,256]{3,2,1,0:T(8,128)} custom-call(f32[5,16,16,256]{3,2,1,0:T(8,128)S(1)} %local.1.local_any.local_ref, f32[16,2,5,2,128]{4,3,2,1,0:T(2,128)S(1)} %all_to_all.10.sums_ref), custom_call_target="tpu_custom_call" | custom-call | tf_op jit(solution)/shard_map/filter/pallas_call | solution.py:440
Async XLA Ops:
  0.6 1.3 %copy-start = (f32[5,16,16,256]{3,2,1,0:T(8,128)S(1)}, f32[5,16,16,256]{3,2,1,0:T(8,128)}, u32[]{:S(2)}) copy-start(f32[5,16,16,256]{3,2,1,0:T(8,128)} %state_any.1) | copy-start | bytes 3932164
  2.3 14.7 %collective-permute-start = (f32[5,4,16,256]{3,2,1,0:T(8,128)S(1)}, f32[5,4,16,256]{3,2,1,0:T(8,128)S(1)}, u32[]{:S(2)}, u32[]{:S(2)}) collective-permute-start(f32[5,4,16,256]{3,2,1,0:T(8,128)S(1)} %get-tuple-element.13), channel_id=1, source_target_pairs={{0,16},{1,17},{2,18},{3,19},{4,20},{5,21},{6,22},{7,23},{8,24},{9,... | collective-permute-start | bytes 983048 | tf_op jit(solution)/shard_map/ppermute | solution.py:379
  5.6 11.4 %collective-permute-start.1 = (f32[5,4,16,256]{3,2,1,0:T(8,128)S(1)}, f32[5,4,16,256]{3,2,1,0:T(8,128)S(1)}, u32[]{:S(2)}, u32[]{:S(2)}) collective-permute-start(f32[5,4,16,256]{3,2,1,0:T(8,128)S(1)} %get-tuple-element.14), channel_id=1, source_target_pairs={{0,240},{1,241},{2,242},{3,243},{4,244},{5,245},{6,246},{7,247},{8... | collective-permute-start | bytes 983048 | tf_op jit(solution)/shard_map/ppermute | solution.py:380
  5.6 11.4 %collective-permute-start.2 = (f32[5,16,4,256]{3,2,1,0:T(4,128)S(1)}, f32[5,16,4,256]{3,2,1,0:T(4,128)S(1)}, u32[]{:S(2)}, u32[]{:S(2)}) collective-permute-start(f32[5,16,4,256]{3,2,1,0:T(4,128)S(1)} %get-tuple-element.15), channel_id=1, source_target_pairs={{0,1},{1,2},{2,3},{3,4},{4,5},{5,6},{6,7},{7,8},{8,9},{9,10},{10,1... | collective-permute-start | bytes 983048 | tf_op jit(solution)/shard_map/ppermute | solution.py:377
  10.5 12.8 %collective-permute-start.3 = (f32[5,16,4,256]{3,2,1,0:T(4,128)S(1)}, f32[5,16,4,256]{3,2,1,0:T(4,128)S(1)}, u32[]{:S(2)}, u32[]{:S(2)}) collective-permute-start(f32[5,16,4,256]{3,2,1,0:T(4,128)S(1)} %get-tuple-element.16), channel_id=1, source_target_pairs={{0,15},{1,0},{2,1},{3,2},{4,3},{5,4},{6,5},{7,6},{8,7},{9,8},{10,9... | collective-permute-start | bytes 983048 | tf_op jit(solution)/shard_map/ppermute | solution.py:378
  10.5 12.8 %copy-start.1 = (f32[5,16,16,256]{3,2,1,0:T(8,128)S(1)}, f32[5,16,16,256]{3,2,1,0:T(8,128)}, u32[]{:S(2)}) copy-start(f32[5,16,16,256]{3,2,1,0:T(8,128)} %register_any.1) | copy-start | bytes 3932164
  27.4 14.2 %all-to-all-start = ((f32[16,2,5,2,128]{4,3,2,1,0:T(2,128)}), f32[16,2,5,2,128]{4,3,2,1,0:T(2,128)S(1)}, u32[]{:S(2)}, u32[]{:S(2)}) async-start(f32[16,2,5,2,128]{4,3,2,1,0:T(2,128)} %get-tuple-element.21), calls=%async_computation | async-start | bytes 327680 | tf_op jit(solution)/shard_map/all_to_all | solution.py:418
  31.6 1.8 %collective-permute-start.4 = (f32[5,2,16,256]{3,2,1,0:T(8,128)S(1)}, f32[5,2,16,256]{3,2,1,0:T(8,128)S(1)}, u32[]{:S(2)}, u32[]{:S(2)}) collective-permute-start(f32[5,2,16,256]{3,2,1,0:T(8,128)S(1)} %get-tuple-element.19), channel_id=1, source_target_pairs={{0,16},{1,17},{2,18},{3,19},{4,20},{5,21},{6,22},{7,23},{8,24},{9,... | collective-permute-start | bytes 491528 | tf_op jit(solution)/shard_map/ppermute | solution.py:419
  31.8 7.9 %collective-permute-start.5 = (f32[5,2,16,256]{3,2,1,0:T(8,128)S(1)}, f32[5,2,16,256]{3,2,1,0:T(8,128)S(1)}, u32[]{:S(2)}, u32[]{:S(2)}) collective-permute-start(f32[5,2,16,256]{3,2,1,0:T(8,128)S(1)} %get-tuple-element.20), channel_id=1, source_target_pairs={{0,240},{1,241},{2,242},{3,243},{4,244},{5,245},{6,246},{7,247},{8... | collective-permute-start | bytes 491528 | tf_op jit(solution)/shard_map/ppermute | solution.py:420

commit v3 on v2

--- a/solution.py
+++ b/solution.py
@@ -2,10 +2,12 @@
 
 import jax
 import jax.numpy as jnp
+import numpy as np
 from jax import lax
 from jax.experimental import pallas as pl
 from jax.experimental.pallas import tpu as pltpu
 from jax.sharding import PartitionSpec as P
+
 
 gamma_gas = 1.4
 central_weights = (4.0 / 5.0, -1.0 / 5.0, 4.0 / 105.0, -1.0 / 280.0)
@@ -80,38 +82,57 @@
             xb_ref[f, step] = state_ref[f, jnp.where(even, 0, 12) + step]
 
 
-def inner_kernel(state_ref, part_ref, prim_ref):
+def difference_matrix():
+    cell = np.arange(256)
+    matrix = np.zeros((256, 256), np.float32)
+    for l, weight in enumerate((672, -168, 32, -3), 1):
+        matrix[(cell + l) % 256, cell] += weight
+        matrix[(cell - l) % 256, cell] -= weight
+    return jnp.asarray(np.concatenate([matrix, matrix]), jnp.bfloat16)
+
+
+def inner_kernel(state_ref, matrix_ref, part_ref, prim_ref):
     row = rows_of((16, 128), 0)
     below = [jnp.where(row < 16 - l, F32(central_weights[l - 1]), F32(0.0)) for l in range(1, 5)]
 
     @pl.loop(0, 16)
     def _(x):
-        prims = [primitives([state_ref[f, x, 8 * half : 8 * half + 8, :] for f in range(5)]) for half in range(2)]
-        along = [[None, None] for _ in range(5)]
-        for half in range(2):
-            own = prims[half]
-            for f in range(6):
-                prim_ref[f, x, 8 * half : 8 * half + 8, :] = own[f]
-            total = [jnp.zeros((8, 256), F32)] * 5
-            for l in range(1, 5):
-                ahead = [pltpu.roll(value, 256 - l, 1) for value in own]
-                flux = pair_flux(own, ahead, 2, central_weights[l - 1])
-                total = [part + (pltpu.roll(value, l, 1) - value) for part, value in zip(total, flux)]
-            for f in range(5):
-                along[f][half] = total[f]
+        state = [state_ref[f, x] for f in range(5)]
+        prims = primitives(state)
+        for f in range(6):
+            prim_ref[f, x] = prims[f]
+        density, speed_x, speed_y, speed_z, pressure, enthalpy = prims
+        momentum = state[3]
+        carried = (speed_x, speed_y, speed_z, enthalpy)
+        dense = (state[1], state[2], state[3], state[4] + pressure)
+        triple = [momentum * value for value in carried]
+        triple[2] = triple[2] + 4.0 * pressure
+        double = [speed_z * value for value in carried]
+        fields = [density, *carried, *dense, *double, *triple]
+        stack = jnp.concatenate(fields, axis=0)
+        high = stack.astype(jnp.bfloat16)
+        low = (stack - high.astype(F32)).astype(jnp.bfloat16)
+        slopes = jnp.dot(
+            jnp.concatenate([high, low], axis=1), matrix_ref[...], preferred_element_type=F32
+        )
+        slopes = [slopes[16 * k : 16 * k + 16] for k in range(17)]
+        mass = slopes[7] + density * slopes[3] + speed_z * slopes[0]
+        along = [(-1.0 / 1680.0) * mass]
+        for k in range(4):
+            value = slopes[13 + k] + density * slopes[9 + k] + speed_z * slopes[5 + k]
+            value = value + momentum * slopes[1 + k] + carried[k] * mass
+            along.append((-1.0 / 3360.0) * value)
         for half in range(2):
             lanes = pl.ds(128 * half, 128)
             cut = slice(128 * half, 128 * half + 128)
-            own = [jnp.concatenate([prims[0][f][:, cut], prims[1][f][:, cut]], axis=0) for f in range(6)]
-            total = [jnp.zeros((16, 128), F32)] * 5
+            own = [value[:, cut] for value in prims]
+            total = [value[:, cut] for value in along]
             for l in range(1, 5):
                 ahead = [pltpu.roll(value, 16 - l, 0) for value in own]
                 flux = pair_flux(own, ahead, 1, below[l - 1])
                 total = [part + (pltpu.roll(value, l, 0) - value) for part, value in zip(total, flux)]
             for f in range(5):
-                part_ref[f, x, :, lanes] = total[f] + jnp.concatenate(
-                    [along[f][0][:, cut], along[f][1][:, cut]], axis=0
-                )
+                part_ref[f, x, :, lanes] = total[f]
 
     for half in range(2):
         lanes = pl.ds(128 * half, 128)
@@ -133,28 +154,13 @@
 
 
 def edge_kernel(
-    even_ref, state_ref, part_ref, register_any, xa_any, xb_any, ya_any, yb_any,
-    out_any, section_any, moment_ref, sa_ref, sb_ref,
-    acc_ref, prim_ref, far_ref, register_ref, xa_ref, xb_ref, ya_ref, yb_ref, out_ref, section_ref,
-    in_sems, out_sems,
+    even_ref, state_ref, part_ref, register_ref, xa_ref, xb_ref, ya_ref, yb_ref,
+    out_any, section_ref, moment_ref, sa_ref, sb_ref,
+    acc_ref, prim_ref, far_ref, out_ref, out_sems,
 ):
     even = even_ref[0] == 1
     row = rows_of((8, 128), 0)
-    arrivals = [
-        pltpu.make_async_copy(source, target, in_sems.at[k])
-        for k, (source, target) in enumerate(
-            ((xa_any, xa_ref), (xb_any, xb_ref), (ya_any, ya_ref), (yb_any, yb_ref), (register_any, register_ref))
-        )
-    ]
-    for copy in arrivals:
-        copy.start()
-    departures = [
-        [
-            pltpu.make_async_copy(out_ref.at[f], out_any.at[f], out_sems.at[0, f]),
-            pltpu.make_async_copy(section_ref.at[f], section_any.at[f], out_sems.at[1, f]),
-        ]
-        for f in range(5)
-    ]
+    departures = [pltpu.make_async_copy(out_ref.at[f], out_any.at[f], out_sems.at[f]) for f in range(5)]
 
     @pl.loop(4, 12)
     def _(x):
@@ -170,9 +176,6 @@
             for f in range(6):
                 prim_ref[0, f, x, rows, :] = first[f]
                 prim_ref[1, f, x, rows, :] = last[f]
-
-    arrivals[0].wait()
-    arrivals[1].wait()
 
     @pl.loop(0, 4)
     def _(x):
@@ -210,9 +213,6 @@
                     total = [part - value for part, value in zip(total, flux)]
                 for f in range(5):
                     acc_ref[f, x + 12, rows, lanes] = total[f]
-
-    arrivals[2].wait()
-    arrivals[3].wait()
 
     @pl.loop(0, 16)
     def _(x):
@@ -238,7 +238,6 @@
                 acc_ref[f, x, 0:8, lanes] = acc_ref[f, x, 0:8, lanes] + jnp.where(row < 4, low[f], 0.0)
                 acc_ref[f, x, 8:16, lanes] = acc_ref[f, x, 8:16, lanes] + jnp.where(row >= 4, high[f], 0.0)
 
-    arrivals[4].wait()
     for f in range(5):
 
         @pl.loop(0, 2)
@@ -259,14 +258,13 @@
                     lanes = slice(128 * half, 128 * half + 128)
                     moment_ref[q, 0, f] = forward[2 * pair : 2 * pair + 2, lanes]
                     moment_ref[q, 1, f] = backward[2 * pair : 2 * pair + 2, lanes]
-        for copy in departures[f]:
-            copy.start()
+
+        departures[f].start()
         for k in range(2):
             sa_ref[f, k] = section_ref[f, jnp.where(even, 14, 0) + k]
             sb_ref[f, k] = section_ref[f, jnp.where(even, 0, 14) + k]
-    for pair in departures:
-        for copy in pair:
-            copy.wait()
+    for copy in departures:
+        copy.wait()
 
 
 def ring_kernel(moment_ref, local_any, sums_ref):
@@ -289,13 +287,9 @@
             value = moment_ref[p, 1, f] + decay * value
 
 
-def local_kernel(even_ref, section_any, xa_ref, xb_ref, out_ref, section_ref, sems):
+def local_kernel(even_ref, section_ref, xa_ref, xb_ref, out_ref):
     even = even_ref[0] == 1
-    arrivals = [pltpu.make_async_copy(section_any.at[f], section_ref.at[f], sems.at[f]) for f in range(5)]
-    for copy in arrivals:
-        copy.start()
     for f in range(5):
-        arrivals[f].wait()
 
         @pl.loop(0, 2)
         def _(tile):
@@ -373,7 +367,7 @@
         scratch_shapes=[pltpu.SemaphoreType.DMA((5,))],
         compiler_params=GRANT,
         name="pack",
-    )(even_flag, state)
+    )(even_flag, pltpu.with_memory_space_constraint(state, pltpu.HBM))
     ya = lax.ppermute(ya, axes, permutation(0, 1))
     yb = lax.ppermute(yb, axes, permutation(0, -1))
     xa = lax.ppermute(xa, axes, permutation(1, 0))
@@ -383,37 +377,30 @@
     part = pl.pallas_call(
         inner_kernel,
         out_shape=pltpu.VMEM(shape, F32),
-        in_specs=[VMEM],
+        in_specs=[VMEM, VMEM],
         out_specs=VMEM,
         scratch_shapes=[pltpu.VMEM((6, 16, 16, 256), F32)],
         compiler_params=GRANT,
         name="inner",
-    )(state)
+    )(state, near(difference_matrix()))
 
     block = jax.ShapeDtypeStruct(shape, F32)
     send = pltpu.VMEM((5, 2, 16, 256), F32)
     register_out, section, moments, sa, sb = pl.pallas_call(
         edge_kernel,
-        out_shape=(block, block, pltpu.VMEM(lines, F32), send, send),
-        in_specs=[SMEM, VMEM, VMEM] + [ANY] * 5,
-        out_specs=(ANY, ANY, VMEM, VMEM, VMEM),
+        out_shape=(block, pltpu.VMEM(shape, F32), pltpu.VMEM(lines, F32), send, send),
+        in_specs=[SMEM] + [VMEM] * 7,
+        out_specs=(pl.BlockSpec(memory_space=pltpu.HBM),) + (VMEM,) * 4,
         scratch_shapes=[
             pltpu.VMEM(shape, F32),
             pltpu.VMEM((2, 6, 4, 16, 256), F32),
             pltpu.VMEM((2, 6, 4, 16, 256), F32),
             pltpu.VMEM(shape, F32),
-            pltpu.VMEM((5, 4, 16, 256), F32),
-            pltpu.VMEM((5, 4, 16, 256), F32),
-            pltpu.VMEM((5, 16, 4, 256), F32),
-            pltpu.VMEM((5, 16, 4, 256), F32),
-            pltpu.VMEM(shape, F32),
-            pltpu.VMEM(shape, F32),
             pltpu.SemaphoreType.DMA((5,)),
-            pltpu.SemaphoreType.DMA((2, 5)),
         ],
         compiler_params=GRANT,
         name="edge",
-    )(even_flag, state, near(part), register, xa, xb, ya, yb)
+    )(even_flag, state, near(part), near(register), near(xa), near(xb), near(ya), near(yb))
 
     moments = lax.all_to_all(moments, "gx", 0, 0, tiled=True)
     sa = lax.ppermute(sa, axes, permutation(1, 0))
@@ -421,12 +408,11 @@
     local = pl.pallas_call(
         local_kernel,
         out_shape=pltpu.VMEM(shape, F32),
-        in_specs=[SMEM, ANY, VMEM, VMEM],
+        in_specs=[SMEM] + [VMEM] * 3,
         out_specs=VMEM,
-        scratch_shapes=[pltpu.VMEM(shape, F32), pltpu.SemaphoreType.DMA((5,))],
         compiler_params=GRANT,
         name="local",
-    )(even_flag, section, sa, sb)
+    )(even_flag, near(section), near(sa), near(sb))
     sums = pl.pallas_call(
         ring_kernel,
         out_shape=pltpu.VMEM(lines, F32),
@@ -455,6 +441,4 @@
 
 def solution(mesh):
     spec = P(None, "gx", "yz", None)
-    return jax.shard_map(
-        body, mesh=mesh, in_specs=(spec, spec), out_specs=(spec, spec), check_vma=False
-    )
+    return jax.shard_map(body, mesh=mesh, in_specs=(spec, spec), out_specs=(spec, spec), check_vma=False)

time: 57.7 us -> 56.6 us (0.981)
  waiting for transfers between devices: 13.6 us -> 14.9 us
  local copies, waits for them, and re-layouts: 1.31 us -> 0.01 us
  Pallas kernels: 13.3 us -> 12.4 us
    unnamed x4, local copies, waits for them, and re-layouts: 1.31 us -> 0.01 us
    pallas_call x1, Pallas kernels: 6.5 us -> 5.32 us  [body(): pl.pallas_call(inner_kernel, out_shape=pltpu.VMEM(shape, F32), in_specs=[...]
    ppermute x1, waiting for transfers between devices: 6.25 us -> 7.43 us  [body(): yb = lax.ppermute(yb, axes, permutation(0, -1))]
    pallas_call x1, Pallas kernels: 0.37 us -> 1.39 us  [body(): pl.pallas_call(pack_kernel, out_shape=(pltpu.VMEM(shape, F32), y_send, y_...]
    pallas_call x1, Pallas kernels: 4.16 us -> 3.52 us  [body(): pl.pallas_call(edge_kernel, out_shape=(block, pltpu.VMEM(shape, F32), plt...]
  transfers between devices with their start and end apart: 7 -> 7, of which waited for: 3 -> 3; matrix products, arithmetic and copies ran while one was open for 0% -> 0% of each run, Pallas kernels for 13% -> 11%
where the time goes in v3:
time: 56.6 us; the launch traced here: 56.4 us
  waiting for transfers between devices  14.9 us (26%)
  blocking collectives  14.3 us (25%)
  starting transfers between devices  14 us (25%)
  Pallas kernels  12.4 us (22%)
  between operations  0.7 us (1%)
    all_to_all x1, blocking collectives, body(): sums = lax.all_to_all(sums, 'gx', 0, 0, tiled=True)  14.3 us
    ppermute x1, waiting for transfers between devices, body(): yb = lax.ppermute(yb, axes, permutation(0, -1))  7.43 us
    ppermute x1, waiting for transfers between devices, body(): sb = lax.ppermute(sb, axes, permutation(-1, 0))  6.31 us
    pallas_call x1, Pallas kernels, body(): pl.pallas_call(inner_kernel, out_shape=pltpu.VMEM(shape, F32), in_specs=[...  5.32 us
    ppermute x1, starting transfers between devices, body(): ya = lax.ppermute(ya, axes, permutation(0, 1))  4.84 us
    all_to_all x1, starting transfers between devices, body(): moments = lax.all_to_all(moments, 'gx', 0, 0, tiled=True)  4.15 us
    pallas_call x1, Pallas kernels, body(): pl.pallas_call(edge_kernel, out_shape=(block, pltpu.VMEM(shape, F32), plt...  3.52 us
    ppermute x1, starting transfers between devices, body(): xa = lax.ppermute(xa, axes, permutation(1, 0))  3.29 us
  transfers between devices with their start and end apart: 7, of which 3 were waited for; matrix products, arithmetic and copies ran while one was open for 0% of the time, Pallas kernels for 11%

profile of v3, /device:TPU:1, one launch (start us, length us, event | category | flops | bytes accessed | tf_op | source)
XLA Modules:
  0.0 56.4 jit_solution(13478073044840679764)
XLA Ops:
  0.6 0.0 copy-start.1
  0.6 1.4 %pack.1 = (f32[5,16,16,256]{3,2,1,0:T(8,128)S(1)}, f32[5,16,4,256]{3,2,1,0:T(4,128)S(1)}, f32[5,16,4,256]{3,2,1,0:T(4,128)S(1)}, f32[5,4,16,256]{3,2,1,0:T(8,128)S(1)}, f32[5,4,16,256]{3,2,1,0:T(8,128)S(1)}) custom-call(s32[1]{0:T(128)} %bitcast.even_ref, f32[5,16,16,256]{3,2,1,0:T(8,128)} %state_any.1), custom_call_target="tpu_custom_call" | custom-call | tf_op jit(solution)/shard_map/pack/pallas_call | solution.py:362
  2.0 3.3 %collective-permute-start = (f32[5,4,16,256]{3,2,1,0:T(8,128)S(1)}, f32[5,4,16,256]{3,2,1,0:T(8,128)S(1)}, u32[]{:S(2)}, u32[]{:S(2)}) collective-permute-start(f32[5,4,16,256]{3,2,1,0:T(8,128)S(1)} %get-tuple-element.13), channel_id=1, source_target_pairs={{0,16},{1,17},{2,18},{3,19},{4,20},{5,21},{6,22},{7,23},{8,24},{9,... | collective-permute-start | bytes 983048 | tf_op jit(solution)/shard_map/ppermute | solution.py:373
  5.3 0.0 collective-permute-start.1
  5.3 4.8 %collective-permute-start.2 = (f32[5,16,4,256]{3,2,1,0:T(4,128)S(1)}, f32[5,16,4,256]{3,2,1,0:T(4,128)S(1)}, u32[]{:S(2)}, u32[]{:S(2)}) collective-permute-start(f32[5,16,4,256]{3,2,1,0:T(4,128)S(1)} %get-tuple-element.15), channel_id=1, source_target_pairs={{0,1},{1,2},{2,3},{3,4},{4,5},{5,6},{6,7},{7,8},{8,9},{9,10},{10,1... | collective-permute-start | bytes 983048 | tf_op jit(solution)/shard_map/ppermute | solution.py:371
  10.2 0.0 collective-permute-start.3
  10.2 0.0 copy-done.1
  10.2 0.0 copy-start
  10.2 5.3 %inner.1.part_ref = f32[5,16,16,256]{3,2,1,0:T(8,128)S(1)} custom-call(f32[5,16,16,256]{3,2,1,0:T(8,128)S(1)} %get-tuple-element.12.state_ref, bf16[512,256]{1,0:T(8,128)(2,1)S(1)} %copy-done.1), custom_call_target="tpu_custom_call" | custom-call | tf_op jit(solution)/shard_map/inner/pallas_call | solution.py:377
  15.5 0.0 collective-permute-done.xa_ref
  15.5 0.0 collective-permute-done.1.xb_ref
  15.5 0.0 collective-permute-done.2.ya_ref
  15.5 7.4 %collective-permute-done.3.yb_ref = f32[5,16,4,256]{3,2,1,0:T(4,128)S(1)} collective-permute-done((f32[5,16,4,256]{3,2,1,0:T(4,128)S(1)}, f32[5,16,4,256]{3,2,1,0:T(4,128)S(1)}, u32[]{:S(2)}, u32[]{:S(2)}) %collective-permute-start.3) | collective-permute-done | bytes 327712 | tf_op jit(solution)/shard_map/ppermute | solution.py:372
  23.0 0.0 copy-done
  23.0 3.5 %edge.1 = (f32[5,16,16,256]{3,2,1,0:T(8,128)}, f32[5,16,16,256]{3,2,1,0:T(8,128)S(1)}, f32[16,2,5,2,128]{4,3,2,1,0:T(2,128)}, f32[5,2,16,256]{3,2,1,0:T(8,128)S(1)}, f32[5,2,16,256]{3,2,1,0:T(8,128)S(1)}) custom-call(s32[1]{0:T(128)} %bitcast.even_ref, f32[5,16,16,256]{3,2,1,0:T(8,128)S(1)} %get-tuple-element.12.state_ref, ...), custom_call_target="tpu_custom_call" | custom-call | tf_op jit(solution)/shard_map/edge/pallas_call | solution.py:389
  26.5 4.1 %all-to-all-start = ((f32[16,2,5,2,128]{4,3,2,1,0:T(2,128)}), f32[16,2,5,2,128]{4,3,2,1,0:T(2,128)S(1)}, u32[]{:S(2)}, u32[]{:S(2)}) async-start(f32[16,2,5,2,128]{4,3,2,1,0:T(2,128)} %get-tuple-element.21), calls=%async_computation | async-start | bytes 327680 | tf_op jit(solution)/shard_map/all_to_all | solution.py:405
  30.7 0.2 collective-permute-start.4
  30.8 1.6 %collective-permute-start.5 = (f32[5,2,16,256]{3,2,1,0:T(8,128)S(1)}, f32[5,2,16,256]{3,2,1,0:T(8,128)S(1)}, u32[]{:S(2)}, u32[]{:S(2)}) collective-permute-start(f32[5,2,16,256]{3,2,1,0:T(8,128)S(1)} %get-tuple-element.20), channel_id=1, source_target_pairs={{0,240},{1,241},{2,242},{3,243},{4,244},{5,245},{6,246},{7,247},{8... | collective-permute-start | bytes 491528 | tf_op jit(solution)/shard_map/ppermute | solution.py:407
  32.4 0.0 collective-permute-done.4.xa_ref
  32.4 6.3 %collective-permute-done.5.xb_ref = f32[5,2,16,256]{3,2,1,0:T(8,128)S(1)} collective-permute-done((f32[5,2,16,256]{3,2,1,0:T(8,128)S(1)}, f32[5,2,16,256]{3,2,1,0:T(8,128)S(1)}, u32[]{:S(2)}, u32[]{:S(2)}) %collective-permute-start.5) | collective-permute-done | bytes 163872 | tf_op jit(solution)/shard_map/ppermute | solution.py:407
  38.7 0.8 %local.1.local_any.local_ref = f32[5,16,16,256]{3,2,1,0:T(8,128)S(1)} custom-call(s32[1]{0:T(128)} %bitcast.even_ref, f32[5,16,16,256]{3,2,1,0:T(8,128)S(1)} %get-tuple-element.18.section_ref, f32[5,2,16,256]{3,2,1,0:T(8,128)S(1)} %collective-permute-done.4.xa_ref, f32[5,2,16,256]{3,2,1,0:T(8,128)S(1)} %collective-permute-done.5.xb_ref), custom_call_target="tpu_custom_call" | custom-call | tf_op jit(solution)/shard_map/local/pallas_call | solution.py:408
  39.5 1.2 %all-to-all-done.moment_ref = f32[16,2,5,2,128]{4,3,2,1,0:T(2,128)S(1)} async-done(((f32[16,2,5,2,128]{4,3,2,1,0:T(2,128)}), f32[16,2,5,2,128]{4,3,2,1,0:T(2,128)S(1)}, u32[]{:S(2)}, u32[]{:S(2)}) %all-to-all-start) | async-done | bytes 163872 | tf_op jit(solution)/shard_map/all_to_all | solution.py:405
  40.7 0.2 ring.1
  40.8 14.3 %all_to_all.10.sums_ref = f32[16,2,5,2,128]{4,3,2,1,0:T(2,128)S(1)} all-to-all(f32[16,2,5,2,128]{4,3,2,1,0:T(2,128)S(1)} %ring.1), channel_id=1, replica_groups=mesh['gx'=16,'yz'=16] {'gx'}, dimensions={0} | all-to-all | bytes 327680 | tf_op jit(solution)/shard_map/all_to_all | solution.py:424
  55.2 1.2 %filter.1 = f32[5,16,16,256]{3,2,1,0:T(8,128)} custom-call(f32[5,16,16,256]{3,2,1,0:T(8,128)S(1)} %local.1.local_any.local_ref, f32[16,2,5,2,128]{4,3,2,1,0:T(2,128)S(1)} %all_to_all.10.sums_ref), custom_call_target="tpu_custom_call" | custom-call | tf_op jit(solution)/shard_map/filter/pallas_call | solution.py:426
Async XLA Ops:
  0.6 9.6 %copy-start.1 = (bf16[512,256]{1,0:T(8,128)(2,1)S(1)}, bf16[512,256]{1,0:T(8,128)(2,1)}, u32[]{:S(2)}) copy-start(bf16[512,256]{1,0:T(8,128)(2,1)} %constant.13.clone.matrix_ref) | copy-start | bytes 786436
  2.0 13.5 %collective-permute-start = (f32[5,4,16,256]{3,2,1,0:T(8,128)S(1)}, f32[5,4,16,256]{3,2,1,0:T(8,128)S(1)}, u32[]{:S(2)}, u32[]{:S(2)}) collective-permute-start(f32[5,4,16,256]{3,2,1,0:T(8,128)S(1)} %get-tuple-element.13), channel_id=1, source_target_pairs={{0,16},{1,17},{2,18},{3,19},{4,20},{5,21},{6,22},{7,23},{8,24},{9,... | collective-permute-start | bytes 983048 | tf_op jit(solution)/shard_map/ppermute | solution.py:373
  5.3 10.2 %collective-permute-start.1 = (f32[5,4,16,256]{3,2,1,0:T(8,128)S(1)}, f32[5,4,16,256]{3,2,1,0:T(8,128)S(1)}, u32[]{:S(2)}, u32[]{:S(2)}) collective-permute-start(f32[5,4,16,256]{3,2,1,0:T(8,128)S(1)} %get-tuple-element.14), channel_id=1, source_target_pairs={{0,240},{1,241},{2,242},{3,243},{4,244},{5,245},{6,246},{7,247},{8... | collective-permute-start | bytes 983048 | tf_op jit(solution)/shard_map/ppermute | solution.py:374
  5.3 10.2 %collective-permute-start.2 = (f32[5,16,4,256]{3,2,1,0:T(4,128)S(1)}, f32[5,16,4,256]{3,2,1,0:T(4,128)S(1)}, u32[]{:S(2)}, u32[]{:S(2)}) collective-permute-start(f32[5,16,4,256]{3,2,1,0:T(4,128)S(1)} %get-tuple-element.15), channel_id=1, source_target_pairs={{0,1},{1,2},{2,3},{3,4},{4,5},{5,6},{6,7},{7,8},{8,9},{9,10},{10,1... | collective-permute-start | bytes 983048 | tf_op jit(solution)/shard_map/ppermute | solution.py:371
  10.2 12.8 %collective-permute-start.3 = (f32[5,16,4,256]{3,2,1,0:T(4,128)S(1)}, f32[5,16,4,256]{3,2,1,0:T(4,128)S(1)}, u32[]{:S(2)}, u32[]{:S(2)}) collective-permute-start(f32[5,16,4,256]{3,2,1,0:T(4,128)S(1)} %get-tuple-element.16), channel_id=1, source_target_pairs={{0,15},{1,0},{2,1},{3,2},{4,3},{5,4},{6,5},{7,6},{8,7},{9,8},{10,9... | collective-permute-start | bytes 983048 | tf_op jit(solution)/shard_map/ppermute | solution.py:372
  10.2 12.8 %copy-start = (f32[5,16,16,256]{3,2,1,0:T(8,128)S(1)}, f32[5,16,16,256]{3,2,1,0:T(8,128)}, u32[]{:S(2)}) copy-start(f32[5,16,16,256]{3,2,1,0:T(8,128)} %register_ref.1) | copy-start | bytes 3932164
  26.5 14.2 %all-to-all-start = ((f32[16,2,5,2,128]{4,3,2,1,0:T(2,128)}), f32[16,2,5,2,128]{4,3,2,1,0:T(2,128)S(1)}, u32[]{:S(2)}, u32[]{:S(2)}) async-start(f32[16,2,5,2,128]{4,3,2,1,0:T(2,128)} %get-tuple-element.21), calls=%async_computation | async-start | bytes 327680 | tf_op jit(solution)/shard_map/all_to_all | solution.py:405
  30.7 1.8 %collective-permute-start.4 = (f32[5,2,16,256]{3,2,1,0:T(8,128)S(1)}, f32[5,2,16,256]{3,2,1,0:T(8,128)S(1)}, u32[]{:S(2)}, u32[]{:S(2)}) collective-permute-start(f32[5,2,16,256]{3,2,1,0:T(8,128)S(1)} %get-tuple-element.19), channel_id=1, source_target_pairs={{0,16},{1,17},{2,18},{3,19},{4,20},{5,21},{6,22},{7,23},{8,24},{9,... | collective-permute-start | bytes 491528 | tf_op jit(solution)/shard_map/ppermute | solution.py:406
  30.8 7.9 %collective-permute-start.5 = (f32[5,2,16,256]{3,2,1,0:T(8,128)S(1)}, f32[5,2,16,256]{3,2,1,0:T(8,128)S(1)}, u32[]{:S(2)}, u32[]{:S(2)}) collective-permute-start(f32[5,2,16,256]{3,2,1,0:T(8,128)S(1)} %get-tuple-element.20), channel_id=1, source_target_pairs={{0,240},{1,241},{2,242},{3,243},{4,244},{5,245},{6,246},{7,247},{8... | collective-permute-start | bytes 491528 | tf_op jit(solution)/shard_map/ppermute | solution.py:407
